TPU v7x, 256 devices: a whole 4x4x8 slice. The times are simulated.
256 devices in a mesh: gx: 4 (over z_lo), gy: 16 (over z_hi, x, core), gz: 4 (over y).
Axes of the slice: x: 4, y: 4, z: 8 (z_hi: 2, z_lo: 4; z = z_hi * 4 + z_lo), core: 2. Of those that a mesh axis runs over, the one named last changes fastest.
Arguments:
- elevation: int32 [512, 512], P('gy', ('gx', 'gz')), may hold values from 0 to 499
- layer_base: float32 [64], P('gz'), may hold values from 0.6 to 1.6
- stretch: float32 [64], P('gz'), may hold values from -0.5 to 0.5
- material: int32 [64, 512, 512], P('gz', 'gy', 'gx'), may hold values from 0 to 15
- buoyancy: float32 [16], replicated, may hold values from 0.5 to 2
- lame_lambda: float32 [16], replicated, may hold values from 0.5 to 2
- shear_modulus: float32 [16], replicated, may hold values from 0.3 to 1.5
- relax_time: float32 [16], replicated, may hold values from 0.2 to 30
- anelastic_weight: float32 [16], replicated, may hold values from 0.05 to 0.5
- velocity: float32 [3, 64, 512, 512], P(None, 'gz', 'gy', 'gx'), may hold values from -6 to 6
- stress: float32 [6, 64, 512, 512], P(None, 'gz', 'gy', 'gx'), may hold values from -6 to 6
- memory: float32 [6, 64, 512, 512], P(None, 'gz', 'gy', 'gx'), may hold values from -4 to 4
Outputs:
- velocity_next: float32 [3, 64, 512, 512], P(None, 'gz', 'gy', 'gx')
- stress_next: float32 [6, 64, 512, 512], P(None, 'gz', 'gy', 'gx')
- memory_next: float32 [6, 64, 512, 512], P(None, 'gz', 'gy', 'gx')
All inputs are finite; a program needn't handle non-finite values.
Results may differ from a plain program's by a relative error of at most 0.00002.
Values sent between devices are 32-bit elements; how exact they have to be, the bound alone decides.
A program may use at most 64 MiB of HBM per device.

v0:
```python
import jax
import jax.numpy as jnp
from jax import lax
from jax.sharding import PartitionSpec as P

step_size = 0.3
binomial = (1.0, 4.0, 6.0, 4.0, 1.0)


def padded_2(value, sides, width):
    for axis, dim in sides:
        size, length = (lax.axis_size(axis), value.shape[dim])
        up = [(i, (i + 1) % size) for i in range(size - 1)]
        down = [(j, i) for i, j in up]
        last = lax.slice_in_dim(value, length - width, length, axis=dim)
        leading = lax.slice_in_dim(value, 0, width, axis=dim)
        before = lax.ppermute(last, axis, up)
        after = lax.ppermute(leading, axis, down)
        value = jnp.concatenate([before, value, after], axis=dim)
    return value


def prefix(value, axis, combine, identity):
    size, mine = (lax.axis_size(axis), lax.axis_index(axis))
    everything = lax.all_gather(value, axis)
    start = jnp.broadcast_to(jnp.asarray(identity, value.dtype), value.shape)

    def step(k, before):
        reached = k < mine
        new = combine(before, everything[k])
        return jnp.where(reached, new, before)

    return lax.fori_loop(0, size, step, start)


def smooth_axis(values_in, dimension):
    length_out = values_in.shape[dimension] - 4
    summed = jnp.zeros_like(lax.slice_in_dim(values_in, 0, length_out, axis=dimension))
    for offset, weight in enumerate(binomial):
        summed = summed + weight * lax.slice_in_dim(
            values_in, offset, offset + length_out, axis=dimension
        )
    return summed / 16.0


def centred(values_in, dimension):
    length_out = values_in.shape[dimension] - 4
    closer = lax.slice_in_dim(values_in, 3, 3 + length_out, axis=dimension) - lax.slice_in_dim(
        values_in, 1, 1 + length_out, axis=dimension
    )
    farther = lax.slice_in_dim(values_in, 4, 4 + length_out, axis=dimension) - lax.slice_in_dim(
        values_in, 0, length_out, axis=dimension
    )
    return (8.0 * closer - farther) / 12.0


def combine_sum(earlier, later):
    return earlier + later


def lookup_table(material, tables):
    stacked = jnp.stack(tables)
    result = jnp.zeros((stacked.shape[0],) + material.shape, jnp.float32)
    for block_id in range(stacked.shape[1]):
        chosen = (material == block_id)[None]
        result = jnp.where(chosen, stacked[:, block_id][:, None, None, None], result)
    return result


def new_velocity(velocity, grad_x, grad_y, grad_k, metric_x, metric_y, metric_z, buoy_cell):
    accel_x = (
        grad_x[0] - metric_x * grad_k[0] + (grad_y[0] - metric_y * grad_k[3]) + metric_z * grad_k[4]
    )
    accel_y = (
        grad_x[1] - metric_x * grad_k[3] + (grad_y[1] - metric_y * grad_k[1]) + metric_z * grad_k[5]
    )
    accel_z = (
        grad_x[2] - metric_x * grad_k[4] + (grad_y[2] - metric_y * grad_k[5]) + metric_z * grad_k[2]
    )
    return velocity + step_size * buoy_cell[None] * jnp.stack([accel_x, accel_y, accel_z])


def new_stress(stress, memory, vel_x, vel_y, vel_k, metric_x, metric_y, metric_z, properties):
    along_x = vel_x - metric_x[None] * vel_k
    along_y = vel_y - metric_y[None] * vel_k
    along_z = metric_z[None] * vel_k
    lame_cell = properties[1]
    shear_cell = properties[2]
    volume_rate = along_x[0] + along_y[1] + along_z[2]
    elastic_rate = jnp.stack(
        [
            lame_cell * volume_rate + 2.0 * shear_cell * along_x[0],
            lame_cell * volume_rate + 2.0 * shear_cell * along_y[1],
            lame_cell * volume_rate + 2.0 * shear_cell * along_z[2],
            shear_cell * (along_y[0] + along_x[1]),
            shear_cell * (along_z[0] + along_x[2]),
            shear_cell * (along_z[1] + along_y[2]),
        ]
    )
    keep_factor = properties[3][None]
    memory_next = keep_factor * memory + (1.0 - keep_factor) * properties[4][None] * elastic_rate
    stress_next = stress + step_size * (elastic_rate - memory_next)
    return (stress_next, memory_next)


def local(
    elevation,
    layer_base,
    stretch,
    material,
    buoyancy,
    lame_lambda,
    shear_modulus,
    relax_time,
    anelastic_weight,
    velocity,
    stress,
    memory,
):
    height = elevation.astype(jnp.float32) / 200.0
    surface_slab = lax.all_gather(height, "gz", axis=1, tiled=True)
    rimmed = padded_2(surface_slab, (("gx", 1), ("gy", 0)), 4)
    surface = smooth_axis(smooth_axis(rimmed, 0), 1)
    slope_x = centred(surface[2:-2, :], 1)
    slope_y = centred(surface[:, 2:-2], 0)
    surface_own = surface[2:-2, 2:-2]
    thickness = layer_base[:, None, None] * jnp.exp(stretch[:, None, None] * surface_own[None])
    weighted = stretch[:, None, None] * thickness
    partial_sum = jnp.sum(weighted, axis=0)
    upper_sum = prefix(partial_sum, "gz", combine_sum, jnp.zeros_like(partial_sum))
    lift = upper_sum[None] + jnp.cumsum(weighted, axis=0) - 0.5 * weighted
    factor = (lift - 1.0) / thickness
    metric_x = slope_x[None] * factor
    metric_y = slope_y[None] * factor
    metric_z = 1.0 / thickness
    properties = lookup_table(
        material,
        (buoyancy, lame_lambda, shear_modulus, jnp.exp(-step_size / relax_time), anelastic_weight),
    )
    padded = padded_2(stress, (("gx", 3), ("gy", 2), ("gz", 1)), 2)
    stress_x = jnp.concatenate([padded[0:1], padded[3:5]])[:, 2:-2, 2:-2, :]
    stress_y = jnp.concatenate([padded[3:4], padded[1:2], padded[5:6]])[:, 2:-2, :, 2:-2]
    stress_z = padded[:, :, 2:-2, 2:-2]
    velocity_next = new_velocity(
        velocity,
        centred(stress_x, 3),
        centred(stress_y, 2),
        centred(stress_z, 1),
        metric_x,
        metric_y,
        metric_z,
        properties[0],
    )
    vel_pad = padded_2(velocity_next, (("gx", 3), ("gy", 2), ("gz", 1)), 2)
    vel_x = centred(vel_pad[:, 2:-2, 2:-2, :], 3)
    vel_y = centred(vel_pad[:, 2:-2, :, 2:-2], 2)
    vel_k = centred(vel_pad[:, :, 2:-2, 2:-2], 1)
    stress_next, memory_next = new_stress(
        stress, memory, vel_x, vel_y, vel_k, metric_x, metric_y, metric_z, properties
    )
    return (velocity_next, stress_next, memory_next)


def solution(mesh):
    return jax.shard_map(
        local,
        mesh=mesh,
        in_specs=(
            P("gy", ("gx", "gz")),
            P("gz"),
            P("gz"),
            P("gz", "gy", "gx"),
            P(),
            P(),
            P(),
            P(),
            P(),
            P(None, "gz", "gy", "gx"),
            P(None, "gz", "gy", "gx"),
            P(None, "gz", "gy", "gx"),
        ),
        out_specs=(P(None, "gz", "gy", "gx"), P(None, "gz", "gy", "gx"), P(None, "gz", "gy", "gx")),
        check_vma=False,
    )
```

profile of v0, /device:TPU:47, one launch (start us, length us, event | category | flops | bytes accessed | tf_op | source)
XLA Modules:
  0.0 173.2 jit_solution(5413824947654246523)
XLA Ops:
  0.6 2.6 %fusion.97 = (f32[6,16,32,2]{3,2,1,0:T(8,128)S(1)}, f32[6,16,32,2]{3,2,1,0:T(8,128)S(1)}) fusion(f32[6,16,32,128]{3,2,1,0:T(8,128)} %param.24), kind=kLoop, calls=%fused_computation.263 | loop fusion | bytes 98304 | tf_op jit(solution)/shard_map/slice | solution.py:15
  3.9 3.7 %collective-permute-start = (f32[6,16,32,2]{2,1,3,0:T(8,128)S(1)}, f32[6,16,32,2]{2,1,3,0:T(8,128)}, u32[]{:S(2)}, u32[]{:S(2)}) collective-permute-start(f32[6,16,32,2]{2,1,3,0:T(8,128)S(1)} %copy.46), channel_id=1, source_target_pairs={{0,64},{64,128},{128,192},{1,65},{65,129},{129,193},{2,66},{66,130... | collective-permute-start | bytes 73736 | tf_op jit(solution)/shard_map/ppermute | solution.py:17
  8.9 2.3 %collective-permute-start.1 = (f32[6,16,32,2]{2,1,3,0:T(8,128)}, f32[6,16,32,2]{2,1,3,0:T(8,128)}, u32[]{:S(2)}, u32[]{:S(2)}) collective-permute-start(f32[6,16,32,2]{2,1,3,0:T(8,128)} %copy.47), channel_id=1, source_target_pairs={{64,0},{128,64},{192,128},{65,1},{129,65},{193,129},{66,2},{130,66... | collective-permute-start | bytes 73736 | tf_op jit(solution)/shard_map/ppermute | solution.py:18
  11.3 9.2 %all_gather.9 = f32[32,128]{0,1:T(8,128)S(1)} all-gather(f32[32,32]{0,1:T(8,128)S(1)} %convert_multiply_fusion), channel_id=1, replica_groups=mesh['gx'=4,'gy'=16,'gz'=4] {'gz'}, dimensions={1}, use_global_device_ids=true | all-gather | bytes 20480 | tf_op jit(solution)/shard_map/all_gather | solution.py:121
  20.5 3.1 %collective-permute-start.6 = (f32[32,4]{0,1:T(4,128)S(1)}, f32[32,4]{0,1:T(4,128)S(1)}, u32[]{:S(2)}, u32[]{:S(2)}) collective-permute-start(f32[32,4]{0,1:T(4,128)S(1)} %get-tuple-element.161), channel_id=1, source_target_pairs={{0,64},{64,128},{128,192},{1,65},{65,129},{129,193},{2,66},{66,130... | collective-permute-start | bytes 1544 | tf_op jit(solution)/shard_map/ppermute | solution.py:17
  23.6 2.1 %collective-permute-start.7 = (f32[32,4]{0,1:T(4,128)S(1)}, f32[32,4]{0,1:T(4,128)S(1)}, u32[]{:S(2)}, u32[]{:S(2)}) collective-permute-start(f32[32,4]{0,1:T(4,128)S(1)} %get-tuple-element.162), channel_id=1, source_target_pairs={{64,0},{128,64},{192,128},{65,1},{129,65},{193,129},{66,2},{130,66... | collective-permute-start | bytes 1544 | tf_op jit(solution)/shard_map/ppermute | solution.py:18
  29.1 12.4 %collective-permute-start.8 = (f32[4,136]{1,0:T(4,128)S(1)}, f32[4,136]{1,0:T(4,128)S(1)}, u32[]{:S(2)}, u32[]{:S(2)}) collective-permute-start(f32[4,136]{1,0:T(4,128)S(1)} %get-tuple-element.163), channel_id=1, source_target_pairs={{0,4},{4,8},{8,12},{12,16},{16,20},{20,24},{24,28},{28,32},{32,36}... | collective-permute-start | bytes 6536 | tf_op jit(solution)/shard_map/ppermute | solution.py:17
  41.5 1.9 %collective-permute-start.9 = (f32[4,136]{1,0:T(4,128)S(1)}, f32[4,136]{1,0:T(4,128)S(1)}, u32[]{:S(2)}, u32[]{:S(2)}) collective-permute-start(f32[4,136]{1,0:T(4,128)S(1)} %get-tuple-element.164), channel_id=1, source_target_pairs={{4,0},{8,4},{12,8},{16,12},{20,16},{24,20},{28,24},{32,28},{36,32}... | collective-permute-start | bytes 6536 | tf_op jit(solution)/shard_map/ppermute | solution.py:18
  44.2 8.3 %collective-permute-done.9 = f32[4,136]{1,0:T(4,128)S(1)} collective-permute-done((f32[4,136]{1,0:T(4,128)S(1)}, f32[4,136]{1,0:T(4,128)S(1)}, u32[]{:S(2)}, u32[]{:S(2)}) %collective-permute-start.9) | collective-permute-done | bytes 2208 | tf_op jit(solution)/shard_map/ppermute | solution.py:18
  55.2 2.7 %copy.35 = f32[6,16,32,2]{3,2,1,0:T(8,128)} copy(f32[6,16,32,2]{2,1,3,0:T(8,128)} %collective-permute-done.1) | data formatting | bytes 49152 | tf_op jit(solution)/shard_map/ppermute | solution.py:18
  59.8 1.9 %collective-permute-start.2 = (f32[6,16,2,132]{3,2,1,0:T(2,128)S(1)}, f32[6,16,2,132]{3,2,1,0:T(2,128)S(1)}, u32[]{:S(2)}, u32[]{:S(2)}) collective-permute-start(f32[6,16,2,132]{3,2,1,0:T(2,128)S(1)} %get-tuple-element.128), channel_id=1, source_target_pairs={{0,4},{4,8},{8,12},{12,16},{16,20},{20,24},{24,28},{28,32},{32,36}... | collective-permute-start | bytes 304136 | tf_op jit(solution)/shard_map/ppermute | solution.py:17
  61.7 2.4 %collective-permute-start.3 = (f32[6,16,2,132]{3,2,1,0:T(2,128)S(1)}, f32[6,16,2,132]{3,2,1,0:T(2,128)S(1)}, u32[]{:S(2)}, u32[]{:S(2)}) collective-permute-start(f32[6,16,2,132]{3,2,1,0:T(2,128)S(1)} %get-tuple-element.129), channel_id=1, source_target_pairs={{4,0},{8,4},{12,8},{16,12},{20,16},{24,20},{28,24},{32,28},{36,32}... | collective-permute-start | bytes 304136 | tf_op jit(solution)/shard_map/ppermute | solution.py:18
  64.3 9.7 %all-gather = f32[128,128]{1,0:T(8,128)} all-gather(f32[32,128]{1,0:T(8,128)S(1)} %fusion.78), channel_id=2, replica_groups=mesh['gx'=4,'gy'=16,'gz'=4] {'gz'}, dimensions={0}, use_global_device_ids=true | all-gather | bytes 81920 | tf_op jit(solution)/shard_map/all_gather | solution.py:25
  74.0 2.9 %collective-permute-done.3 = f32[6,16,2,132]{3,2,1,0:T(2,128)S(1)} collective-permute-done((f32[6,16,2,132]{3,2,1,0:T(2,128)S(1)}, f32[6,16,2,132]{3,2,1,0:T(2,128)S(1)}, u32[]{:S(2)}, u32[]{:S(2)}) %collective-permute-start.3) | collective-permute-done | bytes 101408 | tf_op jit(solution)/shard_map/ppermute | solution.py:18
  80.2 4.3 %collective-permute-start.5 = (f32[6,2,36,132]{3,2,1,0:T(8,128)}, f32[6,2,36,132]{3,2,1,0:T(8,128)}, u32[]{:S(2)}, u32[]{:S(2)}) collective-permute-start(f32[6,2,36,132]{3,2,1,0:T(8,128)} %get-tuple-element.126), channel_id=1, source_target_pairs={{1,0},{2,1},{3,2},{5,4},{6,5},{7,6},{9,8},{10,9},{11,10},{13,12},{... | collective-permute-start | bytes 684296 | tf_op jit(solution)/shard_map/ppermute | solution.py:18
  84.5 2.9 %while.14 = (s32[]{:T(128)}, f32[32,128]{1,0:T(8,128)S(1)}, s32[]{:T(128)}, f32[4,32,128]{2,1,0:T(8,128)}, s32[]{:T(128)}, /*index=5*/s32[]{:T(128)}) while((s32[]{:T(128)}, f32[32,128]{1,0:T(8,128)S(1)}, s32[]{:T(128)}, f32[4,32,128]{2,1,0:T(8,128)}, s32[]{:T(128)}, /*index=5*/s32[]{:T(128)}) %tuple.88), condition=%wide.region_2.3_spmd.clone, body=%wide.region_1.2_spmd.clone.sunk | while | flops 12292 | bytes 49245 | solution.py:33
  87.4 5.8 %collective-permute-done.4 = f32[6,2,36,132]{3,2,1,0:T(8,128)} collective-permute-done((f32[6,2,36,132]{3,2,1,0:T(8,128)}, f32[6,2,36,132]{3,2,1,0:T(8,128)}, u32[]{:S(2)}, u32[]{:S(2)}) %collective-permute-start.4) | collective-permute-done | bytes 228128 | tf_op jit(solution)/shard_map/ppermute | solution.py:17
  93.2 2.5 %collective-permute-done.5 = f32[6,2,36,132]{3,2,1,0:T(8,128)} collective-permute-done((f32[6,2,36,132]{3,2,1,0:T(8,128)}, f32[6,2,36,132]{3,2,1,0:T(8,128)}, u32[]{:S(2)}, u32[]{:S(2)}) %collective-permute-start.5) | collective-permute-done | bytes 228128 | tf_op jit(solution)/shard_map/ppermute | solution.py:18
  95.7 3.4 %pad_maximum_fusion = f32[6,20,36,132]{3,2,1,0:T(8,128)S(1)} fusion(f32[6,2,36,132]{3,2,1,0:T(8,128)} %collective-permute-done.5, f32[6,16,2,132]{3,2,1,0:T(2,128)S(1)} %collective-permute-done.3, f32[6,16,32,2]{3,2,1,0:T(8,128)} %copy.35, f32[6,16,32,128]{3,2,1,0:T(8,128)S(1)} %copy-done, f32[6,16,32,2]{3,2,1,0:T(8,128)S(1)} %copy.34, ...), kind=kLoop, calls=%fused_computation.1 | loop fusion | flops 3421440 | bytes 4561920 | tf_op jit(solution)/shard_map/concatenate | solution.py:19
  100.6 5.3 %fusion.14 = f32[3,20,36,132]{3,2,1,0:T(8,128)S(1)} fusion(f32[6,16,32,2]{3,2,1,0:T(8,128)S(1)} %copy.34, f32[6,16,32,128]{3,2,1,0:T(8,128)S(1)} %copy-done, f32[6,16,32,2]{3,2,1,0:T(8,128)S(1)} %copy-done.2, f32[6,2,36,132]{3,2,1,0:T(8,128)} %collective-permute-done.4, f32[6,2,36,132]{3,2,1,0:T(8,128)} %collective-permute-done.5, ...), kind=kLoop, calls=%fused_computation.46 | loop fusion | flops 13115520 | bytes 3421440 | tf_op jit(solution)/shard_map/concatenate | solution.py:142
  109.1 4.6 %fusion.30 = f32[6,16,32,128]{3,2,1,0:T(8,128)S(1)} fusion(f32[6,2,36,132]{3,2,1,0:T(8,128)} %collective-permute-done.4, f32[6,16,2,132]{3,2,1,0:T(2,128)S(1)} %collective-permute-done.3, f32[6,16,2,132]{3,2,1,0:T(2,128)S(1)} %collective-permute-done.2, f32[6,16,32,2]{3,2,1,0:T(8,128)S(1)} %copy-done.2, f32[6,16,32,128]{3,2,1,0:T(8,128)S(1)} %copy-done, ...), kind=kLoop, calls=%fused_computation.65 | loop fusion | flops 9830400 | bytes 3853824 | tf_op jit(solution)/shard_map/div | solution.py:54
  118.2 1.9 %collective-permute-start.10 = (f32[3,16,32,2]{2,1,3,0:T(8,128)S(1)}, f32[3,16,32,2]{2,1,3,0:T(8,128)S(1)}, u32[]{:S(2)}, u32[]{:S(2)}) collective-permute-start(f32[3,16,32,2]{2,1,3,0:T(8,128)S(1)} %copy.40), channel_id=1, source_target_pairs={{64,0},{128,64},{192,128},{65,1},{129,65},{193,129},{66,2},{130,66... | collective-permute-start | bytes 36872 | tf_op jit(solution)/shard_map/ppermute | solution.py:18
  121.1 3.4 %collective-permute-start.11 = (f32[3,16,32,2]{2,1,3,0:T(8,128)}, f32[3,16,32,2]{2,1,3,0:T(8,128)}, u32[]{:S(2)}, u32[]{:S(2)}) collective-permute-start(f32[3,16,32,2]{2,1,3,0:T(8,128)} %copy.42), channel_id=1, source_target_pairs={{0,64},{64,128},{128,192},{1,65},{65,129},{129,193},{2,66},{66,130... | collective-permute-start | bytes 36872 | tf_op jit(solution)/shard_map/ppermute | solution.py:17
  126.2 2.0 %copy.43 = f32[3,16,32,2]{3,2,1,0:T(8,128)} copy(f32[3,16,32,2]{2,1,3,0:T(8,128)} %collective-permute-done.11) | data formatting | bytes 24576 | tf_op jit(solution)/shard_map/ppermute | solution.py:17
  129.8 7.0 %collective-permute-start.12 = (f32[3,16,2,132]{3,2,1,0:T(2,128)S(1)}, f32[3,16,2,132]{3,2,1,0:T(2,128)S(1)}, u32[]{:S(2)}, u32[]{:S(2)}) collective-permute-start(f32[3,16,2,132]{3,2,1,0:T(2,128)S(1)} %get-tuple-element.134), channel_id=1, source_target_pairs={{0,4},{4,8},{8,12},{12,16},{16,20},{20,24},{24,28},{28,32},{32,36}... | collective-permute-start | bytes 152072 | tf_op jit(solution)/shard_map/ppermute | solution.py:17
  138.7 10.0 %collective-permute-done.13 = f32[3,16,2,132]{3,2,1,0:T(2,128)S(1)} collective-permute-done((f32[3,16,2,132]{3,2,1,0:T(2,128)S(1)}, f32[3,16,2,132]{3,2,1,0:T(2,128)S(1)}, u32[]{:S(2)}, u32[]{:S(2)}) %collective-permute-start.13) | collective-permute-done | bytes 50720 | tf_op jit(solution)/shard_map/ppermute | solution.py:18
  149.0 3.9 %collective-permute-start.14 = (f32[3,2,36,132]{3,2,1,0:T(8,128)S(1)}, f32[3,2,36,132]{3,2,1,0:T(8,128)S(1)}, u32[]{:S(2)}, u32[]{:S(2)}) collective-permute-start(f32[3,2,36,132]{3,2,1,0:T(8,128)S(1)} %get-tuple-element.132), channel_id=1, source_target_pairs={{1,0},{2,1},{3,2},{5,4},{6,5},{7,6},{9,8},{10,9},{11,10},{13,12},{... | collective-permute-start | bytes 342152 | tf_op jit(solution)/shard_map/ppermute | solution.py:18
  152.9 2.1 %collective-permute-start.15 = (f32[3,2,36,132]{3,2,1,0:T(8,128)S(1)}, f32[3,2,36,132]{3,2,1,0:T(8,128)S(1)}, u32[]{:S(2)}, u32[]{:S(2)}) collective-permute-start(f32[3,2,36,132]{3,2,1,0:T(8,128)S(1)} %get-tuple-element.133), channel_id=1, source_target_pairs={{0,1},{1,2},{2,3},{4,5},{5,6},{6,7},{8,9},{9,10},{10,11},{12,13},{... | collective-permute-start | bytes 342152 | tf_op jit(solution)/shard_map/ppermute | solution.py:17
  156.2 3.6 %collective-permute-done.15 = f32[3,2,36,132]{3,2,1,0:T(8,128)S(1)} collective-permute-done((f32[3,2,36,132]{3,2,1,0:T(8,128)S(1)}, f32[3,2,36,132]{3,2,1,0:T(8,128)S(1)}, u32[]{:S(2)}, u32[]{:S(2)}) %collective-permute-start.15) | collective-permute-done | bytes 114080 | tf_op jit(solution)/shard_map/ppermute | solution.py:17
  159.8 4.1 %fusion.42 = f32[3,16,32,128]{3,2,1,0:T(8,128)S(1)} fusion(f32[3,16,2,132]{3,2,1,0:T(2,128)S(1)} %collective-permute-done.12, f32[3,16,32,2]{3,2,1,0:T(8,128)S(1)} %copy.41, f32[3,16,32,128]{3,2,1,0:T(8,128)S(1)} %fusion.54, f32[3,16,32,2]{3,2,1,0:T(8,128)S(1)} %copy-done.4, f32[3,16,2,132]{3,2,1,0:T(2,128)S(1)} %collective-permute-done.13, ...), kind=kLoop, calls=%fused_computation.95 | loop fusion | flops 8454144 | bytes 2189056 | tf_op jit(solution)/shard_map/sub | solution.py:85
  165.0 4.0 %fusion.37 = f32[3,16,32,128]{3,2,1,0:T(8,128)S(1)} fusion(f32[3,16,32,2]{3,2,1,0:T(8,128)S(1)} %copy-done.4, f32[3,16,32,128]{3,2,1,0:T(8,128)S(1)} %fusion.54, f32[3,16,32,2]{3,2,1,0:T(8,128)S(1)} %copy.41, f32[16,32,128]{2,1,0:T(8,128)S(1)} %get-tuple-element.144, f32[3,16,2,132]{3,2,1,0:T(2,128)S(1)} %collective-permute-done.13, ...), kind=kLoop, calls=%fused_computation.89 | loop fusion | flops 6881280 | bytes 2189056 | tf_op jit(solution)/shard_map/sub | solution.py:84
  170.8 2.5 %multiply_add_fusion = (f32[6,16,32,128]{3,2,1,0:T(8,128)}, f32[6,16,32,128]{3,2,1,0:T(8,128)}) fusion(f32[6,16,32,128]{3,2,1,0:T(8,128)S(1)} %copy-done, f32[6,16,32,128]{3,2,1,0:T(8,128)S(1)} %fusion.57, f32[16,32,128]{2,1,0:T(8,128)S(1)} %get-tuple-element.140, f32[6,16,32,128]{3,2,1,0:T(8,128)S(1)} %copy-done.7, f32[16,32,128]{2,1,0:T(8,128)S(1)} %get-tuple-element.138), kind=kLoop, calls=%fused_computation.81 | loop fusion | flops 2359296 | bytes 8388608 | tf_op jit(solution)/shard_map/add | solution.py:102
  (120 shorter events, 36.3 us)
Async XLA Ops:
  3.2 8.0 %copy-start.18 = (s32[32,32]{1,0:T(8,128)S(1)}, s32[32,32]{1,0:T(8,128)}, u32[]{:S(2)}) copy-start(s32[32,32]{1,0:T(8,128)} %param.14) | copy-start | bytes 12292
  3.2 22.6 %copy-start.17 = (s32[16,32,128]{2,1,0:T(8,128)S(1)}, s32[16,32,128]{2,1,0:T(8,128)}, u32[]{:S(2)}) copy-start(s32[16,32,128]{2,1,0:T(8,128)} %param.17) | copy-start | bytes 786436
  3.9 22.6 %copy-start.29 = (f32[16]{0:T(128)S(1)}, f32[16]{0:T(128)}, u32[]{:S(2)}) copy-start(f32[16]{0:T(128)} %param.21) | copy-start | bytes 196
  3.9 49.7 %collective-permute-start = (f32[6,16,32,2]{2,1,3,0:T(8,128)S(1)}, f32[6,16,32,2]{2,1,3,0:T(8,128)}, u32[]{:S(2)}, u32[]{:S(2)}) collective-permute-start(f32[6,16,32,2]{2,1,3,0:T(8,128)S(1)} %copy.46), channel_id=1, source_target_pairs={{0,64},{64,128},{128,192},{1,65},{65,129},{129,193},{2,66},{66,130... | collective-permute-start | bytes 73736 | tf_op jit(solution)/shard_map/ppermute | solution.py:17
  7.5 18.9 %copy-start.25 = (f32[16]{0:T(128)S(1)}, f32[16]{0:T(128)}, u32[]{:S(2)}) copy-start(f32[16]{0:T(128)} %param.18) | copy-start | bytes 196
  7.6 18.9 %copy-start.26 = (f32[16]{0:T(128)S(1)}, f32[16]{0:T(128)}, u32[]{:S(2)}) copy-start(f32[16]{0:T(128)} %param.19) | copy-start | bytes 196
  7.6 18.9 %copy-start.27 = (f32[16]{0:T(128)S(1)}, f32[16]{0:T(128)}, u32[]{:S(2)}) copy-start(f32[16]{0:T(128)} %param.20) | copy-start | bytes 196
  7.6 18.9 %copy-start.28 = (f32[16]{0:T(128)S(1)}, f32[16]{0:T(128)}, u32[]{:S(2)}) copy-start(f32[16]{0:T(128)} %param.22) | copy-start | bytes 196
  8.9 46.3 %collective-permute-start.1 = (f32[6,16,32,2]{2,1,3,0:T(8,128)}, f32[6,16,32,2]{2,1,3,0:T(8,128)}, u32[]{:S(2)}, u32[]{:S(2)}) collective-permute-start(f32[6,16,32,2]{2,1,3,0:T(8,128)} %copy.47), channel_id=1, source_target_pairs={{64,0},{128,64},{192,128},{65,1},{129,65},{193,129},{66,2},{130,66... | collective-permute-start | bytes 73736 | tf_op jit(solution)/shard_map/ppermute | solution.py:18
  20.5 8.4 %collective-permute-start.6 = (f32[32,4]{0,1:T(4,128)S(1)}, f32[32,4]{0,1:T(4,128)S(1)}, u32[]{:S(2)}, u32[]{:S(2)}) collective-permute-start(f32[32,4]{0,1:T(4,128)S(1)} %get-tuple-element.161), channel_id=1, source_target_pairs={{0,64},{64,128},{128,192},{1,65},{65,129},{129,193},{2,66},{66,130... | collective-permute-start | bytes 1544 | tf_op jit(solution)/shard_map/ppermute | solution.py:17
  23.6 5.3 %collective-permute-start.7 = (f32[32,4]{0,1:T(4,128)S(1)}, f32[32,4]{0,1:T(4,128)S(1)}, u32[]{:S(2)}, u32[]{:S(2)}) collective-permute-start(f32[32,4]{0,1:T(4,128)S(1)} %get-tuple-element.162), channel_id=1, source_target_pairs={{64,0},{128,64},{192,128},{65,1},{129,65},{193,129},{66,2},{130,66... | collective-permute-start | bytes 1544 | tf_op jit(solution)/shard_map/ppermute | solution.py:18
  28.8 24.0 %copy-start.5 = (f32[5,16,32,128]{3,2,1,0:T(8,128)}, f32[5,16,32,128]{3,2,1,0:T(8,128)S(1)}, u32[]{:S(2)}) copy-start(f32[5,16,32,128]{3,2,1,0:T(8,128)S(1)} %select_select_fusion) | copy-start | bytes 3932164
  29.1 15.1 %collective-permute-start.8 = (f32[4,136]{1,0:T(4,128)S(1)}, f32[4,136]{1,0:T(4,128)S(1)}, u32[]{:S(2)}, u32[]{:S(2)}) collective-permute-start(f32[4,136]{1,0:T(4,128)S(1)} %get-tuple-element.163), channel_id=1, source_target_pairs={{0,4},{4,8},{8,12},{12,16},{16,20},{20,24},{24,28},{28,32},{32,36}... | collective-permute-start | bytes 6536 | tf_op jit(solution)/shard_map/ppermute | solution.py:17
  41.5 10.9 %collective-permute-start.9 = (f32[4,136]{1,0:T(4,128)S(1)}, f32[4,136]{1,0:T(4,128)S(1)}, u32[]{:S(2)}, u32[]{:S(2)}) collective-permute-start(f32[4,136]{1,0:T(4,128)S(1)} %get-tuple-element.164), channel_id=1, source_target_pairs={{4,0},{8,4},{12,8},{16,12},{20,16},{24,20},{28,24},{32,28},{36,32}... | collective-permute-start | bytes 6536 | tf_op jit(solution)/shard_map/ppermute | solution.py:18
  57.9 19.0 %copy-start.1 = (f32[6,16,32,2]{3,2,1,0:T(8,128)S(1)}, f32[6,16,32,2]{3,2,1,0:T(8,128)}, u32[]{:S(2)}) copy-start(f32[6,16,32,2]{3,2,1,0:T(8,128)} %copy.35) | copy-start | bytes 73732
  59.8 14.2 %collective-permute-start.2 = (f32[6,16,2,132]{3,2,1,0:T(2,128)S(1)}, f32[6,16,2,132]{3,2,1,0:T(2,128)S(1)}, u32[]{:S(2)}, u32[]{:S(2)}) collective-permute-start(f32[6,16,2,132]{3,2,1,0:T(2,128)S(1)} %get-tuple-element.128), channel_id=1, source_target_pairs={{0,4},{4,8},{8,12},{12,16},{16,20},{20,24},{24,28},{28,32},{32,36}... | collective-permute-start | bytes 304136 | tf_op jit(solution)/shard_map/ppermute | solution.py:17
  61.7 15.1 %collective-permute-start.3 = (f32[6,16,2,132]{3,2,1,0:T(2,128)S(1)}, f32[6,16,2,132]{3,2,1,0:T(2,128)S(1)}, u32[]{:S(2)}, u32[]{:S(2)}) collective-permute-start(f32[6,16,2,132]{3,2,1,0:T(2,128)S(1)} %get-tuple-element.129), channel_id=1, source_target_pairs={{4,0},{8,4},{12,8},{16,12},{20,16},{24,20},{28,24},{32,28},{36,32}... | collective-permute-start | bytes 304136 | tf_op jit(solution)/shard_map/ppermute | solution.py:18
  78.3 14.9 %collective-permute-start.4 = (f32[6,2,36,132]{3,2,1,0:T(8,128)}, f32[6,2,36,132]{3,2,1,0:T(8,128)}, u32[]{:S(2)}, u32[]{:S(2)}) collective-permute-start(f32[6,2,36,132]{3,2,1,0:T(8,128)} %get-tuple-element.127), channel_id=1, source_target_pairs={{0,1},{1,2},{2,3},{4,5},{5,6},{6,7},{8,9},{9,10},{10,11},{12,13},{... | collective-permute-start | bytes 684296 | tf_op jit(solution)/shard_map/ppermute | solution.py:17
  80.2 15.5 %collective-permute-start.5 = (f32[6,2,36,132]{3,2,1,0:T(8,128)}, f32[6,2,36,132]{3,2,1,0:T(8,128)}, u32[]{:S(2)}, u32[]{:S(2)}) collective-permute-start(f32[6,2,36,132]{3,2,1,0:T(8,128)} %get-tuple-element.126), channel_id=1, source_target_pairs={{1,0},{2,1},{3,2},{5,4},{6,5},{7,6},{9,8},{10,9},{11,10},{13,12},{... | collective-permute-start | bytes 684296 | tf_op jit(solution)/shard_map/ppermute | solution.py:18
  115.5 49.5 %copy-start.3 = (f32[3,16,32,128]{3,2,1,0:T(8,128)}, f32[3,16,32,128]{3,2,1,0:T(8,128)S(1)}, u32[]{:S(2)}) copy-start(f32[3,16,32,128]{3,2,1,0:T(8,128)S(1)} %fusion.54) | copy-start | bytes 2359300
  118.2 6.3 %collective-permute-start.10 = (f32[3,16,32,2]{2,1,3,0:T(8,128)S(1)}, f32[3,16,32,2]{2,1,3,0:T(8,128)S(1)}, u32[]{:S(2)}, u32[]{:S(2)}) collective-permute-start(f32[3,16,32,2]{2,1,3,0:T(8,128)S(1)} %copy.40), channel_id=1, source_target_pairs={{64,0},{128,64},{192,128},{65,1},{129,65},{193,129},{66,2},{130,66... | collective-permute-start | bytes 36872 | tf_op jit(solution)/shard_map/ppermute | solution.py:18
  121.1 5.1 %collective-permute-start.11 = (f32[3,16,32,2]{2,1,3,0:T(8,128)}, f32[3,16,32,2]{2,1,3,0:T(8,128)}, u32[]{:S(2)}, u32[]{:S(2)}) collective-permute-start(f32[3,16,32,2]{2,1,3,0:T(8,128)} %copy.42), channel_id=1, source_target_pairs={{0,64},{64,128},{128,192},{1,65},{65,129},{129,193},{2,66},{66,130... | collective-permute-start | bytes 36872 | tf_op jit(solution)/shard_map/ppermute | solution.py:17
  128.2 20.5 %copy-start.4 = (f32[3,16,32,2]{3,2,1,0:T(8,128)S(1)}, f32[3,16,32,2]{3,2,1,0:T(8,128)}, u32[]{:S(2)}) copy-start(f32[3,16,32,2]{3,2,1,0:T(8,128)} %copy.43) | copy-start | bytes 36868
  129.7 25.3 %copy-start.12 = (f32[32,128]{1,0:T(8,128)S(1)}, f32[32,128]{1,0:T(8,128)}, u32[]{:S(2)}) copy-start(f32[32,128]{1,0:T(8,128)} %get-tuple-element.167) | copy-start | bytes 49156
  129.7 25.3 %copy-start.14 = (f32[32,128]{1,0:T(8,128)S(1)}, f32[32,128]{1,0:T(8,128)}, u32[]{:S(2)}) copy-start(f32[32,128]{1,0:T(8,128)} %get-tuple-element.165) | copy-start | bytes 49156
  129.7 25.3 %copy-start.16 = (f32[32,128]{1,0:T(8,128)S(1)}, f32[32,128]{1,0:T(8,128)}, u32[]{:S(2)}) copy-start(f32[32,128]{1,0:T(8,128)} %get-tuple-element.166) | copy-start | bytes 49156
  129.8 25.3 %copy-start.21 = (f32[16]{0:T(128)S(1)}, f32[16]{0:T(128)}, u32[]{:S(2)}) copy-start(f32[16]{0:T(128)} %param.16) | copy-start | bytes 196
  129.8 25.3 %copy-start.24 = (f32[16]{0:T(128)S(1)}, f32[16]{0:T(128)}, u32[]{:S(2)}) copy-start(f32[16]{0:T(128)} %param.15) | copy-start | bytes 196
  129.8 8.9 %collective-permute-start.12 = (f32[3,16,2,132]{3,2,1,0:T(2,128)S(1)}, f32[3,16,2,132]{3,2,1,0:T(2,128)S(1)}, u32[]{:S(2)}, u32[]{:S(2)}) collective-permute-start(f32[3,16,2,132]{3,2,1,0:T(2,128)S(1)} %get-tuple-element.134), channel_id=1, source_target_pairs={{0,4},{4,8},{8,12},{12,16},{16,20},{20,24},{24,28},{28,32},{32,36}... | collective-permute-start | bytes 152072 | tf_op jit(solution)/shard_map/ppermute | solution.py:17
  136.8 12.0 %collective-permute-start.13 = (f32[3,16,2,132]{3,2,1,0:T(2,128)S(1)}, f32[3,16,2,132]{3,2,1,0:T(2,128)S(1)}, u32[]{:S(2)}, u32[]{:S(2)}) collective-permute-start(f32[3,16,2,132]{3,2,1,0:T(2,128)S(1)} %get-tuple-element.135), channel_id=1, source_target_pairs={{4,0},{8,4},{12,8},{16,12},{20,16},{24,20},{28,24},{32,28},{36,32}... | collective-permute-start | bytes 152072 | tf_op jit(solution)/shard_map/ppermute | solution.py:18
  149.0 7.2 %collective-permute-start.14 = (f32[3,2,36,132]{3,2,1,0:T(8,128)S(1)}, f32[3,2,36,132]{3,2,1,0:T(8,128)S(1)}, u32[]{:S(2)}, u32[]{:S(2)}) collective-permute-start(f32[3,2,36,132]{3,2,1,0:T(8,128)S(1)} %get-tuple-element.132), channel_id=1, source_target_pairs={{1,0},{2,1},{3,2},{5,4},{6,5},{7,6},{9,8},{10,9},{11,10},{13,12},{... | collective-permute-start | bytes 342152 | tf_op jit(solution)/shard_map/ppermute | solution.py:18
  152.9 6.9 %collective-permute-start.15 = (f32[3,2,36,132]{3,2,1,0:T(8,128)S(1)}, f32[3,2,36,132]{3,2,1,0:T(8,128)S(1)}, u32[]{:S(2)}, u32[]{:S(2)}) collective-permute-start(f32[3,2,36,132]{3,2,1,0:T(8,128)S(1)} %get-tuple-element.133), channel_id=1, source_target_pairs={{0,1},{1,2},{2,3},{4,5},{5,6},{6,7},{8,9},{9,10},{10,11},{12,13},{... | collective-permute-start | bytes 342152 | tf_op jit(solution)/shard_map/ppermute | solution.py:17
  (14 other events, 55.3 us)
where the time goes:
time: 174 us; the launch traced here: 173 us
  starting transfers between devices  56.4 us (32%)
  other arithmetic  41.9 us (24%)
  waiting for transfers between devices  35.4 us (20%)
  local copies, waits for them, and re-layouts  19.2 us (11%)
  blocking collectives  18.9 us (11%)
    ppermute x8, starting transfers between devices, padded_2(): before = lax.ppermute(last, axis, up)  35.5 us
    ppermute x8, waiting for transfers between devices, padded_2(): after = lax.ppermute(leading, axis, down)  24.6 us
    ppermute x8, starting transfers between devices, padded_2(): after = lax.ppermute(leading, axis, down)  20.8 us
    ppermute x8, waiting for transfers between devices, padded_2(): before = lax.ppermute(last, axis, up)  10.8 us
    all_gather x1, blocking collectives, prefix(): everything = lax.all_gather(value, axis)  9.71 us
    all_gather x1, blocking collectives, local(): surface_slab = lax.all_gather(height, 'gz', axis=1, tiled=True)  9.19 us
    div x3, other arithmetic, centred(): return (8.0 * closer - farther) / 12.0  6.76 us
    unnamed x63, local copies, waits for them, and re-layouts  5.54 us
  transfers between devices with their start and end apart: 16, of which 8 were waited for; matrix products, arithmetic and copies ran while one was open for 7% of the time, Pallas kernels for 0%

commit v1 on v0

v1 whole, which is shorter than its diff:
```python
import functools

import jax
import jax.numpy as jnp
from jax import lax
from jax.experimental import pallas as pl
from jax.experimental.pallas import tpu as pltpu
from jax.sharding import PartitionSpec as P

MESH = pl.DeviceIdType.MESH
STEP = 0.3
GX, GY, GZ = 4, 16, 4
NZ, NY, NX = 16, 32, 128
X_PARTS = (0, 3, 4)
Y_PARTS = (3, 1, 5)
Y_SENT = (1, 3, 5)
BLOCK = 16


def when(condition, action):
    if condition is None:
        action()
    else:
        pl.when(condition)(lambda: action())


def centred_12(before_2, before_1, after_1, after_2):
    return 8.0 * (after_1 - before_1) - (after_2 - before_2)


def kernel(
    elevation, layer_base, stretch, material, buoyancy, lame, shear, relax, weight, velocity, stress, memory,
    v_out, s_out, m_out,
    sigma, vel, terrain, wide, surf, slopes, layers, mat, tables, metric, packs, halo_s, halo_v,
    small, local_sem, s_send, s_recv, v_send, v_recv, y_send, y_recv, layer_send, layer_recv, t_send, t_recv,
):
    x, y, z = lax.axis_index("gx"), lax.axis_index("gy"), lax.axis_index("gz")
    x_low, x_high = x > 0, x < GX - 1
    y_low, y_high = y > 0, y < GY - 1
    z_low, z_high = z > 0, z < GZ - 1
    lane = lax.broadcasted_iota(jnp.int32, (8, NX), 1)

    own_slot = 1 + z
    tables_in = (buoyancy, lame, shear, relax, weight, layer_base, stretch)
    scalars = [pltpu.make_async_copy(ref, small.at[i], local_sem.at[i]) for i, ref in enumerate(tables_in)]
    for copy in scalars:
        copy.start()
    stress_in = {
        c: pltpu.make_async_copy(stress.at[c], sigma.at[c, 2:18, 8:40, :], local_sem.at[7 + c])
        for c in (0, 3, 4, 1, 2, 5)
    }
    for c in (0, 3, 4, 1, 2, 5):
        stress_in[c].start()
    elevation_in = pltpu.make_async_copy(elevation, terrain.at[own_slot, 8:40, :], local_sem.at[13])
    velocity_in = pltpu.make_async_copy(velocity, v_out, local_sem.at[14])
    material_in = pltpu.make_async_copy(material, mat, local_sem.at[15])
    memory_in = pltpu.make_async_copy(memory, m_out, local_sem.at[16])
    for copy in (elevation_in, material_in, velocity_in, memory_in):
        copy.start()

    barrier = pltpu.get_barrier_semaphore()
    partners = [(None, {"gz": (z + d) % GZ}) for d in range(1, GZ)]
    partners += [(y_low, {"gy": y - 1}), (y_high, {"gy": y + 1})]
    for g in range(GZ):
        partners.append((x_high & ((z == g) | (z == GZ - 1) | (g == 0)), {"gx": x + 1, "gz": g}))
        partners.append((x_low & ((z == g) | (z == 0) | (g == GZ - 1)), {"gx": x - 1, "gz": g}))
    for condition, target in partners:
        when(condition, lambda target=target: pl.semaphore_signal(barrier, inc=1, device_id=target, device_id_type=MESH))

    for copy in scalars:
        copy.wait()
    for k in range(NZ):
        for row in range(2):
            layers[row, pl.ds(NZ * z + k, 1), :] = jnp.full((1, NX), small[5 + row, k], jnp.float32)
    columns = []
    for i in range(5):
        column = jnp.zeros((8, NX), jnp.float32)
        for block_id in range(16):
            column = jnp.where(lane == block_id, small[i, block_id], column)
        columns.append(column)
    keep = jnp.exp(-STEP / jnp.where(lane < 16, columns[3], 1.0))
    tables[0] = columns[0] * (STEP / 12.0)
    tables[1] = columns[1] * (1.0 / 12.0)
    tables[2] = columns[2] * (1.0 / 12.0)
    tables[3] = keep
    tables[4] = (1.0 - keep) * columns[4]

    def zero_stress_z(first):
        sigma[:, pl.ds(first, 2), 8:40, :] = jnp.zeros((6, 2, NY, NX), jnp.float32)
        vel[:, pl.ds(first, 2), 8:40, :] = jnp.zeros((3, 2, NY, NX), jnp.float32)

    def zero_y(first):
        def layer(k, carry):
            for c in Y_SENT:
                sigma[c, 2 + k, first : first + 8, :] = jnp.zeros((8, NX), jnp.float32)
            for c in range(3):
                vel[c, 2 + k, first : first + 8, :] = jnp.zeros((8, NX), jnp.float32)
            return carry

        lax.fori_loop(0, NZ, layer, 0)
        for m in range(6):
            terrain[m, first : first + 8, :] = jnp.zeros((8, 32), jnp.int32)

    def zero_x(side, slot):
        halo_s[side] = jnp.zeros((2, NY, NX), jnp.float32)
        halo_v[side] = jnp.zeros((2, NY, NX), jnp.float32)
        terrain[slot] = jnp.zeros((48, 32), jnp.int32)

    when(z == 0, lambda: zero_stress_z(0))
    when(z == GZ - 1, lambda: zero_stress_z(18))
    when(y == 0, lambda: zero_y(0))
    when(y == GY - 1, lambda: zero_y(40))
    when(x == 0, lambda: zero_x(0, 0))
    when(x == GX - 1, lambda: zero_x(1, 5))

    def pack(parts, field, phase):
        def layer(k, held):
            held = list(held)
            for i, c in enumerate(parts):
                at = 4 * (k + (NZ if i == 1 else 0))
                spot = (lane >= at) & (lane < at + 4)
                for r in range(4):
                    rolled = pltpu.roll(field[c, 2 + k, 8 + 8 * r : 16 + 8 * r, :], at + 2, 1)
                    j = 4 * (i // 2) + r
                    held[j] = jnp.where(spot, rolled, held[j])
            return tuple(held)

        held = lax.fori_loop(0, NZ, layer, tuple(jnp.zeros((8, NX), jnp.float32) for _ in range(8)))
        for j in range(8):
            packs[phase, j // 4, 8 * (j % 4) : 8 * (j % 4) + 8, :] = held[j]

    for c in X_PARTS:
        stress_in[c].wait()
    pack(X_PARTS, sigma, 0)

    pl.semaphore_wait(barrier, sum(1 if c is None else c.astype(jnp.int32) for c, _ in partners))

    def remote(source, to, send, recv, target):
        return pltpu.make_async_remote_copy(
            src_ref=source, dst_ref=to, send_sem=send, recv_sem=recv, device_id=target, device_id_type=MESH
        )

    sends = []

    def send(condition, copy):
        sends.append((condition, copy))
        when(condition, copy.start)

    up_y, down_y = {"gy": y + 1}, {"gy": y - 1}
    low_rows, high_rows = terrain.at[own_slot, 0:8, :], terrain.at[own_slot, 40:48, :]
    send(y_high, remote(elevation.at[24:32, :], low_rows, t_send.at[1, 7], t_recv.at[own_slot, 1], up_y))
    send(y_low, remote(elevation.at[0:8, :], high_rows, t_send.at[2, 7], t_recv.at[own_slot, 2], down_y))
    for i, c in enumerate(Y_SENT):
        send(y_high, remote(stress.at[c, :, 30:32, :], sigma.at[c, 2:18, 6:8, :], y_send.at[0, i], y_recv.at[0, i], up_y))
        send(y_low, remote(stress.at[c, :, 0:2, :], sigma.at[c, 2:18, 40:42, :], y_send.at[1, i], y_recv.at[1, i], down_y))

    def spread(part, source, rows, condition):
        def both(other):
            return other if condition is None else (condition if other is None else condition & other)

        for d in range(1, GZ):
            g = (z + d) % GZ
            send(both(None), remote(source, terrain.at[own_slot, rows, :], t_send.at[part, d - 1], t_recv.at[own_slot, part], {"gz": g}))
        for g in range(GZ):
            send(both(x_high & (z == GZ - 1)), remote(source, terrain.at[0, rows, :], t_send.at[part, 3 + g], t_recv.at[0, part], {"gx": x + 1, "gz": g}))
            send(both(x_low & (z == 0)), remote(source, terrain.at[5, rows, :], t_send.at[part, 3 + g], t_recv.at[5, part], {"gx": x - 1, "gz": g}))

    spread(0, elevation, slice(8, 40), None)
    mine = pl.ds(NZ * z, NZ)
    for d in range(1, GZ):
        send(None, remote(layers.at[:, mine, :], layers.at[:, mine, :], layer_send.at[d - 1], layer_recv.at[z], {"gz": (z + d) % GZ}))
    send(x_high, remote(packs.at[0], halo_s.at[0], s_send.at[0], s_recv.at[0], {"gx": x + 1}))
    send(x_low, remote(packs.at[0], halo_s.at[1], s_send.at[1], s_recv.at[1], {"gx": x - 1}))
    send(z_high, remote(stress.at[:, 14:16], sigma.at[:, 0:2, 8:40, :], s_send.at[2], s_recv.at[2], {"gz": z + 1}))
    send(z_low, remote(stress.at[:, 0:2], sigma.at[:, 18:20, 8:40, :], s_send.at[3], s_recv.at[3], {"gz": z - 1}))

    def arrived(ref, recv):
        remote(ref, ref, s_send.at[0], recv, {"gz": z}).wait_recv()

    when(y_low, lambda: arrived(low_rows, t_recv.at[own_slot, 1]))
    when(y_high, lambda: arrived(high_rows, t_recv.at[own_slot, 2]))
    spread(1, low_rows, slice(0, 8), y_low)
    spread(2, high_rows, slice(40, 48), y_high)

    elevation_in.wait()

    def slot_arrived(slot, condition):
        def both(other):
            return other if condition is None else (condition if other is None else condition & other)

        when(both(None), lambda: arrived(terrain.at[slot, 8:40, :], t_recv.at[slot, 0]))
        when(both(y_low), lambda: arrived(terrain.at[slot, 0:8, :], t_recv.at[slot, 1]))
        when(both(y_high), lambda: arrived(terrain.at[slot, 40:48, :], t_recv.at[slot, 2]))

    for d in range(1, GZ):
        g = (z + d) % GZ
        slot_arrived(1 + g, None)
        arrived(layers.at[:, pl.ds(NZ * g, NZ), :], layer_recv.at[g])
    slot_arrived(0, x_low)
    slot_arrived(5, x_high)

    for r in range(6):
        rows = slice(8 * r, 8 * r + 8)
        held = [terrain[m, rows, :].astype(jnp.float32) / 200.0 for m in range(6)]
        blank = jnp.zeros((8, 96), jnp.float32)
        wide[0, rows, :] = jnp.concatenate([blank, held[0]], axis=1)
        wide[1, rows, :] = jnp.concatenate(held[1:5], axis=1)
        wide[2, rows, :] = jnp.concatenate([held[5], blank], axis=1)
    binomial = (1.0, 4.0, 6.0, 4.0, 1.0)
    along_y = []
    for part in range(3):
        total = jnp.zeros((40, NX), jnp.float32)
        for d, factor in enumerate(binomial):
            total = total + factor * wide[part, 2 + d : 42 + d, :]
        along_y.append(total / 16.0)
    row = jnp.concatenate(along_y, axis=1)
    total = jnp.zeros_like(row)
    for d, factor in enumerate(binomial):
        total = total + factor * (row if d == 2 else pltpu.roll(row, (2 - d) % 384, 1))
    total = total / 16.0
    for part in range(3):
        surf[part] = total[:, 128 * part : 128 * part + 128]
    own = jnp.concatenate([surf[part, 4:36, :] for part in range(3)], axis=1)
    shifted = [pltpu.roll(own, d % 384, 1)[:, 128:256] for d in (2, 1, -1, -2)]
    slopes[0] = centred_12(*shifted) / 12.0
    slopes[1] = centred_12(*[surf[1, 4 + d : 36 + d, :] for d in (-2, -1, 1, 2)]) / 12.0

    def metrics(first, rows):
        at = slice(first, first + rows)
        height = surf[1, 4 + first : 4 + first + rows, :]
        slope_x, slope_y = slopes[0, at, :], slopes[1, at, :]

        def above(layer, total):
            base, follow = layers[0, pl.ds(layer, 1), :], layers[1, pl.ds(layer, 1), :]
            return total + follow * (base * jnp.exp(follow * height))

        upper = lax.fori_loop(0, NZ * z, above, jnp.zeros((rows, NX), jnp.float32))

        def layer(k, total):
            base, follow = layers[0, pl.ds(NZ * z + k, 1), :], layers[1, pl.ds(NZ * z + k, 1), :]
            thickness = base * jnp.exp(follow * height)
            weighted = follow * thickness
            inverse = 1.0 / thickness
            factor = (total + 0.5 * weighted - 1.0) * inverse
            metric[0, k, at, :] = slope_x * factor
            metric[1, k, at, :] = slope_y * factor
            metric[2, k, at, :] = inverse
            return total + weighted

        lax.fori_loop(0, NZ, layer, upper)

    for first in range(0, NY, BLOCK):
        metrics(first, BLOCK)

    side = lax.broadcasted_iota(jnp.int32, (BLOCK, NX), 1)

    def d_k(field, c, k, first):
        at = slice(8 + first, 8 + first + BLOCK)
        return centred_12(*[field[c, k + 2 + d, at, :] for d in (-2, -1, 1, 2)])

    def d_y(field, c, k, first):
        return centred_12(*[field[c, k + 2, 8 + first + d : 8 + first + d + BLOCK, :] for d in (-2, -1, 1, 2)])

    def d_x(field, c, k, first, halo, i):
        here = field[c, k + 2, 8 + first : 8 + first + BLOCK, :]
        at = 4 * (k + (NZ if i == 1 else 0))
        beside = pltpu.roll(halo[0, i // 2, first : first + BLOCK, :], 126 - at, 1)
        return centred_12(
            pltpu.roll(jnp.where(side >= 126, beside, here), 2, 1), pltpu.roll(jnp.where(side >= 127, beside, here), 1, 1),
            pltpu.roll(jnp.where(side < 1, beside, here), 127, 1), pltpu.roll(jnp.where(side < 2, beside, here), 126, 1),
        )

    def join(halo):
        for i in range(2):
            for r in range(4):
                rows = slice(8 * r, 8 * r + 8)
                halo[0, i, rows, :] = jnp.where(lane % 4 < 2, halo[0, i, rows, :], halo[1, i, rows, :])

    def look_up(i, block_id):
        table = jnp.concatenate([tables[i]] * (BLOCK // 8), axis=0)
        return jnp.take_along_axis(table, block_id, axis=1)

    for copy in (stress_in[1], stress_in[2], stress_in[5], velocity_in, material_in):
        copy.wait()
    when(x_low, lambda: arrived(halo_s.at[0], s_recv.at[0]))
    when(x_high, lambda: arrived(halo_s.at[1], s_recv.at[1]))
    join(halo_s)
    when(z_low, lambda: arrived(sigma.at[:, 0:2, 8:40, :], s_recv.at[2]))
    when(z_high, lambda: arrived(sigma.at[:, 18:20, 8:40, :], s_recv.at[3]))
    for i, c in enumerate(Y_SENT):
        when(y_low, lambda: arrived(sigma.at[c, 2:18, 6:8, :], y_recv.at[0, i]))
        when(y_high, lambda: arrived(sigma.at[c, 2:18, 40:42, :], y_recv.at[1, i]))

    def velocity_layer(k, carry):
        for first in range(0, NY, BLOCK):
            at = slice(first, first + BLOCK)
            m_x, m_y, m_z = (metric[i, k, at, :] for i in range(3))
            grad_k = [d_k(sigma, c, k, first) for c in range(6)]
            grad_x = [d_x(sigma, c, k, first, halo_s, i) for i, c in enumerate(X_PARTS)]
            grad_y = [d_y(sigma, c, k, first) for c in Y_PARTS]
            scale = look_up(0, mat[k, at, :])
            for c, (a, b, d) in enumerate(((0, 3, 4), (3, 1, 5), (4, 5, 2))):
                accel = (grad_x[c] - m_x * grad_k[a]) + (grad_y[c] - m_y * grad_k[b]) + m_z * grad_k[d]
                new = v_out[c, k, at, :] + scale * accel
                v_out[c, k, at, :] = new
                vel[c, 2 + k, 8 + first : 8 + first + BLOCK, :] = new
        return carry

    lax.fori_loop(0, NZ, velocity_layer, 0)
    send(y_high, remote(vel.at[:, 2:18, 38:40, :], vel.at[:, 2:18, 6:8, :], v_send.at[4], v_recv.at[4], up_y))
    send(y_low, remote(vel.at[:, 2:18, 8:10, :], vel.at[:, 2:18, 40:42, :], v_send.at[5], v_recv.at[5], down_y))
    send(z_high, remote(vel.at[:, 16:18, 8:40, :], vel.at[:, 0:2, 8:40, :], v_send.at[2], v_recv.at[2], {"gz": z + 1}))
    send(z_low, remote(vel.at[:, 2:4, 8:40, :], vel.at[:, 18:20, 8:40, :], v_send.at[3], v_recv.at[3], {"gz": z - 1}))
    pack((0, 1, 2), vel, 1)
    send(x_high, remote(packs.at[1], halo_v.at[0], v_send.at[0], v_recv.at[0], {"gx": x + 1}))
    send(x_low, remote(packs.at[1], halo_v.at[1], v_send.at[1], v_recv.at[1], {"gx": x - 1}))

    memory_in.wait()
    when(x_low, lambda: arrived(halo_v.at[0], v_recv.at[0]))
    when(x_high, lambda: arrived(halo_v.at[1], v_recv.at[1]))
    join(halo_v)
    when(z_low, lambda: arrived(vel.at[:, 0:2, 8:40, :], v_recv.at[2]))
    when(z_high, lambda: arrived(vel.at[:, 18:20, 8:40, :], v_recv.at[3]))
    when(y_low, lambda: arrived(vel.at[:, 2:18, 6:8, :], v_recv.at[4]))
    when(y_high, lambda: arrived(vel.at[:, 2:18, 40:42, :], v_recv.at[5]))

    def stress_layer(k, carry):
        for first in range(0, NY, BLOCK):
            at = slice(first, first + BLOCK)
            m_x, m_y, m_z = (metric[i, k, at, :] for i in range(3))
            along_k = [d_k(vel, c, k, first) for c in range(3)]
            along_x = [d_x(vel, c, k, first, halo_v, c) - m_x * along_k[c] for c in range(3)]
            along_y = [d_y(vel, c, k, first) - m_y * along_k[c] for c in range(3)]
            along_z = [m_z * along_k[c] for c in range(3)]
            block_id = mat[k, at, :]
            lam, mu, kept, gain = (look_up(i, block_id) for i in range(1, 5))
            volume = lam * (along_x[0] + along_y[1] + along_z[2])
            twice = mu + mu
            rates = (
                volume + twice * along_x[0],
                volume + twice * along_y[1],
                volume + twice * along_z[2],
                mu * (along_y[0] + along_x[1]),
                mu * (along_z[0] + along_x[2]),
                mu * (along_z[1] + along_y[2]),
            )
            for c, rate in enumerate(rates):
                new = kept * m_out[c, k, at, :] + gain * rate
                m_out[c, k, at, :] = new
                s_out[c, k, at, :] = sigma[c, 2 + k, 8 + first : 8 + first + BLOCK, :] + STEP * (rate - new)
        return carry

    lax.fori_loop(0, NZ, stress_layer, 0)
    for condition, copy in sends:
        when(condition, copy.wait_send)


def local(*arrays):
    held = [pltpu.with_memory_space_constraint(array, pltpu.HBM) for array in arrays]
    f32, vmem, dma = jnp.float32, pltpu.VMEM, pltpu.SemaphoreType.DMA
    outputs = [(n, NZ, NY, NX) for n in (3, 6, 6)]
    return pl.pallas_call(
        kernel,
        out_shape=tuple(vmem(shape, f32) for shape in outputs),
        in_specs=[pl.BlockSpec(memory_space=pltpu.HBM)] * len(held),
        out_specs=tuple(pl.BlockSpec(memory_space=vmem) for _ in outputs),
        scratch_shapes=[
            vmem((6, 20, 48, NX), f32),
            vmem((3, 20, 48, NX), f32),
            vmem((6, 48, 32), jnp.int32),
            vmem((3, 48, NX), f32),
            vmem((3, 40, NX), f32),
            vmem((2, NY, NX), f32),
            vmem((2, GZ * NZ, NX), f32),
            vmem((NZ, NY, NX), jnp.int32),
            vmem((5, 8, NX), f32),
            vmem((3, NZ, NY, NX), f32),
            vmem((2, 2, NY, NX), f32),
            vmem((2, 2, NY, NX), f32),
            vmem((2, 2, NY, NX), f32),
            pltpu.SMEM((7, 16), f32),
            dma((17,)), dma((4,)), dma((4,)), dma((6,)), dma((6,)), dma((2, 3)), dma((2, 3)),
            dma((3,)), dma((4,)), dma((3, 8)), dma((6, 3)),
        ],
        compiler_params=pltpu.CompilerParams(
            collective_id=0, has_side_effects=True, vmem_limit_bytes=24 << 20
        ),
    )(*held)


def solution(mesh):
    field = P(None, "gz", "gy", "gx")
    return jax.shard_map(
        local,
        mesh=mesh,
        in_specs=(
            P("gy", ("gx", "gz")), P("gz"), P("gz"), P("gz", "gy", "gx"),
            P(), P(), P(), P(), P(), field, field, field,
        ),
        out_specs=(field, field, field),
        check_vma=False,
    )
```

time: 174 us -> 36.3 us (0.21)
  the two profiles are of different devices: /device:TPU:47 before, /device:TPU:7 now
where the time goes in v1:
time: 36.3 us; the launch traced here: 36.2 us
  Pallas kernels  32.4 us (89%)
  local copies, waits for them, and re-layouts  3.17 us (9%)
  between operations  0.64 us (2%)
    pallas_call x1, Pallas kernels, local(): pl.pallas_call(kernel, out_shape=tuple((vmem(shape, f32) for shape in out...  32.4 us
    unnamed x3, local copies, waits for them, and re-layouts  3.17 us

profile of v1, /device:TPU:7, one launch (start us, length us, event | category | flops | bytes accessed | tf_op | source)
XLA Modules:
  0.0 36.2 jit_solution(6842888918934224146)
XLA Ops:
  0.6 32.4 %shard_map.139 = (f32[3,16,32,128]{3,2,1,0:T(8,128)S(1)}, f32[6,16,32,128]{3,2,1,0:T(8,128)S(1)}, f32[6,16,32,128]{3,2,1,0:T(8,128)S(1)}) custom-call(s32[32,32]{1,0:T(8,128)} %elevation.1, f32[16]{0:T(128)} %layer_base.1, f32[16]{0:T(128)} %stretch.1, s32[16,32,128]{2,1,0:T(8,128)} %material.1, f32[16]{0:T(128)} %buoyancy.1, f32[16]{0:T(128)} %lame.1, ...), custom_call_target="tpu_custom_call" | custom-call | tf_op jit(solution)/shard_map/pallas_call | solution.py:362
  33.1 0.9 %copy.18 = f32[3,16,32,128]{3,2,1,0:T(8,128)} copy(f32[3,16,32,128]{3,2,1,0:T(8,128)S(1)} %get-tuple-element.3) | data formatting | bytes 1572864
  33.9 1.1 %copy.19 = f32[6,16,32,128]{3,2,1,0:T(8,128)} copy(f32[6,16,32,128]{3,2,1,0:T(8,128)S(1)} %get-tuple-element.4) | data formatting | bytes 3145728
  35.1 1.1 %copy.20 = f32[6,16,32,128]{3,2,1,0:T(8,128)} copy(f32[6,16,32,128]{3,2,1,0:T(8,128)S(1)} %get-tuple-element.5) | data formatting | bytes 3145728

commit v2 on v1

v2 whole, which is shorter than its diff:
```python
import functools

import jax
import jax.numpy as jnp
from jax import lax
from jax.experimental import pallas as pl
from jax.experimental.pallas import tpu as pltpu
from jax.sharding import PartitionSpec as P

MESH = pl.DeviceIdType.MESH
STEP = 0.3
GX, GY, GZ = 4, 16, 4
NZ, NY, NX = 16, 32, 128
X_PARTS = (0, 3, 4)
Y_PARTS = (3, 1, 5)
Y_SENT = (1, 3, 5)


def when(condition, action):
    if condition is None:
        action()
    else:
        pl.when(condition)(lambda: action())


def centred_12(before_2, before_1, after_1, after_2):
    return 8.0 * (after_1 - before_1) - (after_2 - before_2)


def kernel(
    elevation, layer_base, stretch, material, buoyancy, lame, shear, relax, weight, velocity, stress, memory,
    v_out, s_out, m_out,
    sigma, vel, terrain, wide, surf, layers, mat, tables, metric, packs, halo_s, halo_v,
    small, local_sem, s_send, s_recv, y_send, y_recv, layer_send, layer_recv, t_send, t_recv, edge_send, edge_recv,
    z_send, z_recv, x_send, x_recv, vy_send, vy_recv, far_sem,
):
    x, y, z = lax.axis_index("gx"), lax.axis_index("gy"), lax.axis_index("gz")
    x_low, x_high = x > 0, x < GX - 1
    y_low, y_high = y > 0, y < GY - 1
    z_low, z_high = z > 0, z < GZ - 1
    before_gap, after_gap = y == GY // 2 - 1, y == GY // 2
    lane = lax.broadcasted_iota(jnp.int32, (8, NX), 1)

    own_slot = 1 + z
    tables_in = (buoyancy, lame, shear, relax, weight, layer_base, stretch)
    scalars = [pltpu.make_async_copy(ref, small.at[i], local_sem.at[i]) for i, ref in enumerate(tables_in)]
    for copy in scalars:
        copy.start()
    stress_in = {
        c: pltpu.make_async_copy(stress.at[c], sigma.at[c, 2:18, 8:40, :], local_sem.at[7 + c])
        for c in (0, 3, 4, 1, 2, 5)
    }
    for c in (0, 3, 4, 1, 2, 5):
        stress_in[c].start()
    elevation_in = pltpu.make_async_copy(elevation, terrain.at[own_slot, 8:40, :], local_sem.at[13])
    velocity_in = pltpu.make_async_copy(velocity, v_out, local_sem.at[14])
    material_in = pltpu.make_async_copy(material, mat, local_sem.at[15])
    memory_in = pltpu.make_async_copy(memory, m_out, local_sem.at[16])
    for copy in (elevation_in, material_in, velocity_in, memory_in):
        copy.start()

    barrier = pltpu.get_barrier_semaphore()
    beside = [(None, {"gz": (z + d) % GZ}) for d in range(1, GZ)]
    for g in range(GZ):
        beside.append((x_high & ((z == g) | (z == GZ - 1) | (g == 0)), {"gx": x + 1, "gz": g}))
        beside.append((x_low & ((z == g) | (z == 0) | (g == GZ - 1)), {"gx": x - 1, "gz": g}))
    up_y, down_y = {"gy": y + 1}, {"gy": y - 1}
    for condition, target in [(y_high, up_y), (y_low & ~after_gap, down_y)] + beside:
        when(condition, lambda target=target: pl.semaphore_signal(barrier, inc=1, device_id=target, device_id_type=MESH))
    expected = [y_low, y_high & ~before_gap] + [condition for condition, _ in beside]

    for copy in scalars:
        copy.wait()
    for k in range(NZ):
        for row in range(2):
            layers[row, pl.ds(NZ * z + k, 1), :] = jnp.full((1, NX), small[5 + row, k], jnp.float32)

    def pack_spot(k, i):
        at = 4 * (k + (NZ if i == 1 else 0))
        return at, (lane >= at) & (lane < at + 4)

    def pack_layer(held, blocks, i, k, at, spot):
        for r, block in enumerate(blocks):
            j = len(blocks) * (i // 2) + r
            held[j] = jnp.where(spot, pltpu.roll(block, at + 2, 1), held[j])

    def pack_stress(step, held):
        held = list(held)
        for k in (2 * step, 2 * step + 1):
            for i, c in enumerate(X_PARTS):
                at, spot = pack_spot(k, i)
                pack_layer(held, [sigma[c, 2 + k, 8 + 8 * r : 16 + 8 * r, :] for r in range(4)], i, k, at, spot)
        return tuple(held)

    for c in X_PARTS:
        stress_in[c].wait()
    zero = jnp.zeros((8, NX), jnp.float32)
    held = lax.fori_loop(0, NZ // 2, pack_stress, (zero,) * 8)
    for j in range(8):
        packs[0, j // 4, 8 * (j % 4) : 8 * (j % 4) + 8, :] = held[j]

    pl.semaphore_wait(barrier, sum(1 if c is None else c.astype(jnp.int32) for c in expected))
    when(after_gap, lambda: pl.semaphore_signal(far_sem, inc=1, device_id=down_y, device_id_type=MESH))

    def remote(source, to, send, recv, target):
        return pltpu.make_async_remote_copy(
            src_ref=source, dst_ref=to, send_sem=send, recv_sem=recv, device_id=target, device_id_type=MESH
        )

    sends = []

    def send(condition, copy, now=True):
        sends.append((condition, copy))
        if now:
            when(condition, copy.start)
        return copy

    up_copies = [
        send(y_high, remote(stress.at[c, :, 30:32, :], sigma.at[c, 2:18, 6:8, :], y_send.at[0, i], y_recv.at[0, i], up_y), now=False)
        for i, c in enumerate(Y_SENT)
    ]

    def start_up():
        for copy in up_copies:
            copy.start()

    when(y_high & ~before_gap, start_up)
    for d in range(1, GZ):
        send(None, remote(elevation, terrain.at[own_slot, 8:40, :], t_send.at[d - 1], t_recv.at[own_slot], {"gz": (z + d) % GZ}))
    for g in range(GZ):
        send(x_high & (z == GZ - 1), remote(elevation, terrain.at[0, 8:40, :], t_send.at[3 + g], t_recv.at[0], {"gx": x + 1, "gz": g}))
        send(x_low & (z == 0), remote(elevation, terrain.at[5, 8:40, :], t_send.at[3 + g], t_recv.at[5], {"gx": x - 1, "gz": g}))
    mine = pl.ds(NZ * z, NZ)
    for d in range(1, GZ):
        send(None, remote(layers.at[:, mine, :], layers.at[:, mine, :], layer_send.at[d - 1], layer_recv.at[z], {"gz": (z + d) % GZ}))
    for i, c in enumerate(Y_SENT):
        send(y_low, remote(stress.at[c, :, 0:2, :], sigma.at[c, 2:18, 40:42, :], y_send.at[1, i], y_recv.at[1, i], down_y))
    send(x_high, remote(packs.at[0], halo_s.at[0], s_send.at[0], s_recv.at[0], {"gx": x + 1}))
    send(x_low, remote(packs.at[0], halo_s.at[1], s_send.at[1], s_recv.at[1], {"gx": x - 1}))
    send(z_high, remote(stress.at[:, 14:16], sigma.at[:, 0:2, 8:40, :], s_send.at[2], s_recv.at[2], {"gz": z + 1}))
    send(z_low, remote(stress.at[:, 0:2], sigma.at[:, 18:20, 8:40, :], s_send.at[3], s_recv.at[3], {"gz": z - 1}))

    def arrived(ref, recv):
        remote(ref, ref, s_send.at[0], recv, {"gz": z}).wait_recv()

    columns = []
    for i in range(5):
        column = zero
        for block_id in range(16):
            column = jnp.where(lane == block_id, small[i, block_id], column)
        columns.append(column)
    keep = jnp.exp(-STEP / jnp.where(lane < 16, columns[3], 1.0))
    tables[0] = columns[0] * (STEP / 12.0)
    tables[1] = columns[1] * (1.0 / 12.0)
    tables[2] = columns[2] * (1.0 / 12.0)
    tables[3] = keep
    tables[4] = (1.0 - keep) * columns[4]

    def zero_z(first):
        sigma[:, pl.ds(first, 2), 8:40, :] = jnp.zeros((6, 2, NY, NX), jnp.float32)
        vel[:, pl.ds(first, 2), 8:40, :] = jnp.zeros((3, 2, NY, NX), jnp.float32)

    def zero_y(first):
        def layer(k, carry):
            for c in Y_SENT:
                sigma[c, 2 + k, first : first + 8, :] = zero
            for c in range(3):
                vel[c, 2 + k, first : first + 8, :] = zero
            return carry

        lax.fori_loop(0, NZ, layer, 0)
        for m in range(6):
            terrain[m, first : first + 8, :] = jnp.zeros((8, 32), jnp.int32)

    def zero_x(side, slot):
        halo_s[side] = jnp.zeros((2, NY, NX), jnp.float32)
        halo_v[side] = jnp.zeros((2, NY, NX), jnp.float32)
        terrain[slot, 8:40, :] = jnp.zeros((32, 32), jnp.int32)

    when(z == 0, lambda: zero_z(0))
    when(z == GZ - 1, lambda: zero_z(18))
    when(y == 0, lambda: zero_y(0))
    when(y == GY - 1, lambda: zero_y(40))
    when(x == 0, lambda: zero_x(0, 0))
    when(x == GX - 1, lambda: zero_x(1, 5))

    elevation_in.wait()
    for d in range(1, GZ):
        g = (z + d) % GZ
        arrived(terrain.at[1 + g, 8:40, :], t_recv.at[1 + g])
    when(x_low, lambda: arrived(terrain.at[0, 8:40, :], t_recv.at[0]))
    when(x_high, lambda: arrived(terrain.at[5, 8:40, :], t_recv.at[5]))
    edge_up = send(y_high, remote(terrain.at[:, 32:40, :], terrain.at[:, 0:8, :], edge_send.at[0], edge_recv.at[0], up_y), now=False)
    when(y_high & ~before_gap, edge_up.start)
    send(y_low, remote(terrain.at[:, 8:16, :], terrain.at[:, 40:48, :], edge_send.at[1], edge_recv.at[1], down_y))

    def heights(row):
        rows = pl.ds(row, 8)
        held = [terrain[m, rows, :].astype(jnp.float32) / 200.0 for m in range(6)]
        blank = jnp.zeros((8, 96), jnp.float32)
        wide[0, rows, :] = jnp.concatenate([blank, held[0]], axis=1)
        wide[1, rows, :] = jnp.concatenate(held[1:5], axis=1)
        wide[2, rows, :] = jnp.concatenate([held[5], blank], axis=1)

    binomial = (1.0, 4.0, 6.0, 4.0, 1.0)

    def metrics(first, rows):
        along_y = []
        for part in range(3):
            total = jnp.zeros((rows + 8, NX), jnp.float32)
            for d, factor in enumerate(binomial):
                total = total + factor * wide[part, pl.ds(first + 2 + d, rows + 8), :]
            along_y.append(total / 16.0)
        row = jnp.concatenate(along_y, axis=1)
        total = jnp.zeros_like(row)
        for d, factor in enumerate(binomial):
            total = total + factor * (row if d == 2 else pltpu.roll(row, (2 - d) % 384, 1))
        total = total / 16.0
        for part in range(3):
            surf[part, 0 : rows + 8, :] = total[:, 128 * part : 128 * part + 128]
        own = jnp.concatenate([surf[part, 4 : 4 + rows, :] for part in range(3)], axis=1)
        height = own[:, 128:256]
        shifted = [pltpu.roll(own, d % 384, 1)[:, 128:256] for d in (2, 1, -1, -2)]
        slope_x = centred_12(*shifted) / 12.0
        slope_y = centred_12(*[surf[1, 4 + d : 4 + d + rows, :] for d in (-2, -1, 1, 2)]) / 12.0

        def above(step, total):
            for layer in [4 * step + i for i in range(4)]:
                base, follow = layers[0, pl.ds(layer, 1), :], layers[1, pl.ds(layer, 1), :]
                total = total + follow * (base * jnp.exp(follow * height))
            return total

        upper = lax.fori_loop(0, (NZ // 4) * z, above, jnp.zeros((rows, NX), jnp.float32))

        def layer(step, total):
            for k in [4 * step + i for i in range(4)]:
                base, follow = layers[0, pl.ds(NZ * z + k, 1), :], layers[1, pl.ds(NZ * z + k, 1), :]
                thickness = base * jnp.exp(follow * height)
                weighted = follow * thickness
                inverse = 1.0 / thickness
                factor = (total + 0.5 * weighted - 1.0) * inverse
                at = pl.ds(first, rows)
                metric[0, k, at, :] = slope_x * factor
                metric[1, k, at, :] = slope_y * factor
                metric[2, k, at, :] = inverse
                total = total + weighted
            return total

        lax.fori_loop(0, NZ // 4, layer, upper)

    def d_k(field, c, k, first, rows):
        return centred_12(*[field[c, k + 2 + d, pl.ds(8 + first, rows), :] for d in (-2, -1, 1, 2)])

    def d_y(field, c, k, first, rows):
        return centred_12(*[field[c, k + 2, pl.ds(8 + first + d, rows), :] for d in (-2, -1, 1, 2)])

    def d_x(field, c, k, first, rows, halo, i):
        side = lax.broadcasted_iota(jnp.int32, (rows, NX), 1)
        here = field[c, k + 2, pl.ds(8 + first, rows), :]
        at = 4 * (k + (NZ if i == 1 else 0))
        beyond = pltpu.roll(halo[0, i // 2, pl.ds(first, rows), :], 126 - at, 1)
        return centred_12(
            pltpu.roll(jnp.where(side >= 126, beyond, here), 2, 1), pltpu.roll(jnp.where(side >= 127, beyond, here), 1, 1),
            pltpu.roll(jnp.where(side < 1, beyond, here), 127, 1), pltpu.roll(jnp.where(side < 2, beyond, here), 126, 1),
        )

    def join(halo, first, rows):
        side = lax.broadcasted_iota(jnp.int32, (rows, NX), 1)
        for i in range(2):
            at = pl.ds(first, rows)
            halo[0, i, at, :] = jnp.where(side % 4 < 2, halo[0, i, at, :], halo[1, i, at, :])

    def look_up(i, block_id):
        table = jnp.concatenate([tables[i]] * (block_id.shape[0] // 8), axis=0)
        return jnp.take_along_axis(table, block_id, axis=1)

    def velocity_rows(first, rows, unroll):
        blocks = rows // 8

        def velocity_layer(step, held):
            held = list(held)
            at = pl.ds(first, rows)
            for k in [unroll * step + i for i in range(unroll)]:
                m_x, m_y, m_z = (metric[i, k, at, :] for i in range(3))
                grad_k = [d_k(sigma, c, k, first, rows) for c in range(6)]
                grad_x = [d_x(sigma, c, k, first, rows, halo_s, i) for i, c in enumerate(X_PARTS)]
                grad_y = [d_y(sigma, c, k, first, rows) for c in Y_PARTS]
                scale = look_up(0, mat[k, at, :])
                for c, (a, b, d) in enumerate(((0, 3, 4), (3, 1, 5), (4, 5, 2))):
                    accel = (grad_x[c] - m_x * grad_k[a]) + (grad_y[c] - m_y * grad_k[b]) + m_z * grad_k[d]
                    new = v_out[c, k, at, :] + scale * accel
                    v_out[c, k, at, :] = new
                    vel[c, 2 + k, pl.ds(8 + first, rows), :] = new
                    spot_at, spot = pack_spot(k, c)
                    pack_layer(held, [new[8 * r : 8 * r + 8] for r in range(blocks)], c, k, spot_at, spot)
            return tuple(held)

        held = lax.fori_loop(0, NZ // unroll, velocity_layer, (zero,) * (2 * blocks))
        for j in range(2 * blocks):
            packs[1, j // blocks, pl.ds(first + 8 * (j % blocks), 8), :] = held[j]

    def send_rows(part, first, rows):
        at = pl.ds(first, rows)
        send(x_high, remote(packs.at[1, :, at, :], halo_v.at[0, :, at, :], x_send.at[0, part], x_recv.at[0, part], {"gx": x + 1}))
        send(x_low, remote(packs.at[1, :, at, :], halo_v.at[1, :, at, :], x_send.at[1, part], x_recv.at[1, part], {"gx": x - 1}))
        at = pl.ds(8 + first, rows)
        send(z_high, remote(vel.at[:, 16:18, at, :], vel.at[:, 0:2, at, :], z_send.at[0, part], z_recv.at[0, part], {"gz": z + 1}))
        send(z_low, remote(vel.at[:, 2:4, at, :], vel.at[:, 18:20, at, :], z_send.at[1, part], z_recv.at[1, part], {"gz": z - 1}))

    def wait_x(part, first, rows):
        at = pl.ds(first, rows)
        when(x_low, lambda: arrived(halo_v.at[0, :, at, :], x_recv.at[0, part]))
        when(x_high, lambda: arrived(halo_v.at[1, :, at, :], x_recv.at[1, part]))
        join(halo_v, first, rows)

    def wait_z(part, first, rows):
        at = pl.ds(8 + first, rows)
        when(z_low, lambda: arrived(vel.at[:, 0:2, at, :], z_recv.at[0, part]))
        when(z_high, lambda: arrived(vel.at[:, 18:20, at, :], z_recv.at[1, part]))

    for row in range(8, 40, 8):
        heights(row)
    for d in range(1, GZ):
        g = (z + d) % GZ
        arrived(layers.at[:, pl.ds(NZ * g, NZ), :], layer_recv.at[g])
    metrics(8, 16)

    def start_far():
        pl.semaphore_wait(far_sem, 1)
        edge_up.start()
        start_up()

    when(before_gap, start_far)
    for copy in (stress_in[1], stress_in[2], stress_in[5], velocity_in, material_in):
        copy.wait()
    when(x_low, lambda: arrived(halo_s.at[0], s_recv.at[0]))
    when(x_high, lambda: arrived(halo_s.at[1], s_recv.at[1]))
    join(halo_s, 0, NY)
    when(z_low, lambda: arrived(sigma.at[:, 0:2, 8:40, :], s_recv.at[2]))
    when(z_high, lambda: arrived(sigma.at[:, 18:20, 8:40, :], s_recv.at[3]))
    velocity_rows(8, 16, 2)
    send_rows(0, 8, 16)

    odd = y % 2
    strips = []
    for part in (1, 2):
        low = (odd == 1) if part == 1 else (odd == 0)
        side = odd if part == 1 else 1 - odd
        strips.append((part, low, pl.multiple_of(24 - 24 * side, 8), pl.multiple_of(40 - 40 * side, 8)))
    low_copy = remote(vel.at[:, 2:18, 8:10, :], vel.at[:, 2:18, 40:42, :], vy_send.at[1], vy_recv.at[1], down_y)
    high_copy = remote(vel.at[:, 2:18, 38:40, :], vel.at[:, 2:18, 6:8, :], vy_send.at[0], vy_recv.at[0], up_y)
    sends.append((y_low, low_copy))
    sends.append((y_high, high_copy))
    for part, low, first, outer in strips:
        when(low & y_low, lambda: arrived(terrain.at[:, 0:8, :], edge_recv.at[0]))
        when(~low & y_high, lambda: arrived(terrain.at[:, 40:48, :], edge_recv.at[1]))
        heights(outer)
        metrics(first, 8)
        for i, c in enumerate(Y_SENT):
            when(low & y_low, lambda: arrived(sigma.at[c, 2:18, 6:8, :], y_recv.at[0, i]))
            when(~low & y_high, lambda: arrived(sigma.at[c, 2:18, 40:42, :], y_recv.at[1, i]))
        velocity_rows(first, 8, 4)
        when(low & y_low, low_copy.start)
        when(~low & y_high, high_copy.start)
        send_rows(part, first, 8)

    memory_in.wait()

    def stress_rows(first, rows, ks):
        at = pl.ds(first, rows)
        for k in ks:
            m_x, m_y, m_z = (metric[i, k, at, :] for i in range(3))
            along_k = [d_k(vel, c, k, first, rows) for c in range(3)]
            along_x = [d_x(vel, c, k, first, rows, halo_v, c) - m_x * along_k[c] for c in range(3)]
            along_y = [d_y(vel, c, k, first, rows) - m_y * along_k[c] for c in range(3)]
            along_z = [m_z * along_k[c] for c in range(3)]
            block_id = mat[k, at, :]
            lam, mu, kept, gain = (look_up(i, block_id) for i in range(1, 5))
            volume = lam * (along_x[0] + along_y[1] + along_z[2])
            twice = mu + mu
            rates = (
                volume + twice * along_x[0],
                volume + twice * along_y[1],
                volume + twice * along_z[2],
                mu * (along_y[0] + along_x[1]),
                mu * (along_z[0] + along_x[2]),
                mu * (along_z[1] + along_y[2]),
            )
            for c, rate in enumerate(rates):
                new = kept * m_out[c, k, at, :] + gain * rate
                m_out[c, k, at, :] = new
                s_out[c, k, at, :] = sigma[c, 2 + k, pl.ds(8 + first, rows), :] + STEP * (rate - new)

    def inner(step, carry):
        stress_rows(8, 16, (2 * step, 2 * step + 1))
        return carry

    wait_x(0, 8, 16)
    lax.fori_loop(1, NZ // 2 - 1, inner, 0)
    wait_z(0, 8, 16)
    lax.fori_loop(0, 2, lambda step, carry: inner(step * (NZ // 2 - 1), carry), 0)
    for part, low, first, outer in strips:
        wait_x(part, first, 8)
        wait_z(part, first, 8)
        when(low & y_low, lambda: arrived(vel.at[:, 2:18, 6:8, :], vy_recv.at[0]))
        when(~low & y_high, lambda: arrived(vel.at[:, 2:18, 40:42, :], vy_recv.at[1]))

        def strip(step, carry):
            stress_rows(first, 8, [4 * step + i for i in range(4)])
            return carry

        lax.fori_loop(0, NZ // 4, strip, 0)
    for condition, copy in sends:
        when(condition, copy.wait_send)


def write_out(v_in, s_in, m_in, v_ref, s_ref, m_ref, sems):
    copies = [pltpu.make_async_copy(v_in, v_ref, sems.at[0])]
    for half in range(2):
        rows = slice(3 * half, 3 * half + 3)
        copies.append(pltpu.make_async_copy(s_in.at[rows], s_ref.at[rows], sems.at[1 + half]))
        copies.append(pltpu.make_async_copy(m_in.at[rows], m_ref.at[rows], sems.at[3 + half]))
    for copy in copies:
        copy.start()
    for copy in copies:
        copy.wait()


def local(*arrays):
    held = [pltpu.with_memory_space_constraint(array, pltpu.HBM) for array in arrays]
    f32, vmem, dma = jnp.float32, pltpu.VMEM, pltpu.SemaphoreType.DMA
    outputs = [(n, NZ, NY, NX) for n in (3, 6, 6)]
    results = pl.pallas_call(
        kernel,
        out_shape=tuple(vmem(shape, f32) for shape in outputs),
        in_specs=[pl.BlockSpec(memory_space=pltpu.HBM)] * len(held),
        out_specs=tuple(pl.BlockSpec(memory_space=vmem) for _ in outputs),
        scratch_shapes=[
            vmem((6, 20, 48, NX), f32),
            vmem((3, 20, 48, NX), f32),
            vmem((6, 48, 32), jnp.int32),
            vmem((3, 48, NX), f32),
            vmem((3, 24, NX), f32),
            vmem((2, GZ * NZ, NX), f32),
            vmem((NZ, NY, NX), jnp.int32),
            vmem((5, 8, NX), f32),
            vmem((3, NZ, NY, NX), f32),
            vmem((2, 2, NY, NX), f32),
            vmem((2, 2, NY, NX), f32),
            vmem((2, 2, NY, NX), f32),
            pltpu.SMEM((7, 16), f32),
            dma((17,)), dma((4,)), dma((4,)), dma((2, 3)), dma((2, 3)), dma((3,)), dma((4,)), dma((7,)), dma((6,)), dma((2,)), dma((2,)),
            dma((2, 3)), dma((2, 3)), dma((2, 3)), dma((2, 3)), dma((2,)), dma((2,)),
            pltpu.SemaphoreType.REGULAR,
        ],
        compiler_params=pltpu.CompilerParams(
            collective_id=0, has_side_effects=True, vmem_limit_bytes=24 << 20
        ),
    )(*held)
    return pl.pallas_call(
        write_out,
        out_shape=tuple(jax.ShapeDtypeStruct(shape, f32) for shape in outputs),
        in_specs=[pl.BlockSpec(memory_space=vmem)] * 3,
        out_specs=tuple(pl.BlockSpec(memory_space=pltpu.HBM) for _ in outputs),
        scratch_shapes=[dma((5,))],
        compiler_params=pltpu.CompilerParams(vmem_limit_bytes=8 << 20),
    )(*results)


def solution(mesh):
    field = P(None, "gz", "gy", "gx")
    return jax.shard_map(
        local,
        mesh=mesh,
        in_specs=(
            P("gy", ("gx", "gz")), P("gz"), P("gz"), P("gz", "gy", "gx"),
            P(), P(), P(), P(), P(), field, field, field,
        ),
        out_specs=(field, field, field),
        check_vma=False,
    )
```

time: 36.3 us -> 29.7 us (0.82)
  the two profiles are of different devices: /device:TPU:7 before, /device:TPU:15 now
where the time goes in v2:
time: 29.7 us
  Pallas kernels  29 us (98%)
  between operations  0.64 us (2%)
    pallas_call x1, Pallas kernels, local(): pl.pallas_call(kernel, out_shape=tuple((vmem(shape, f32) for shape in out...  27.1 us
    pallas_call x1, Pallas kernels, local(): pl.pallas_call(write_out, out_shape=tuple((jax.ShapeDtypeStruct(shape, f3...  1.96 us

profile of v2, /device:TPU:15, one launch (start us, length us, event | category | flops | bytes accessed | tf_op | source)
XLA Modules:
  0.0 29.7 jit_solution(12324173008431172306)
XLA Ops:
  0.6 27.1 %shard_map.139 = (f32[3,16,32,128]{3,2,1,0:T(8,128)S(1)}, f32[6,16,32,128]{3,2,1,0:T(8,128)S(1)}, f32[6,16,32,128]{3,2,1,0:T(8,128)S(1)}) custom-call(s32[32,32]{1,0:T(8,128)} %elevation.1, f32[16]{0:T(128)} %layer_base.1, f32[16]{0:T(128)} %stretch.1, s32[16,32,128]{2,1,0:T(8,128)} %material.1, f32[16]{0:T(128)} %buoyancy.1, f32[16]{0:T(128)} %lame.1, ...), custom_call_target="tpu_custom_call" | custom-call | tf_op jit(solution)/shard_map/pallas_call | solution.py:433
  27.7 2.0 %shard_map.140 = (f32[3,16,32,128]{3,2,1,0:T(8,128)}, f32[6,16,32,128]{3,2,1,0:T(8,128)}, f32[6,16,32,128]{3,2,1,0:T(8,128)}) custom-call(f32[3,16,32,128]{3,2,1,0:T(8,128)S(1)} %get-tuple-element.6.v_in, f32[6,16,32,128]{3,2,1,0:T(8,128)S(1)} %get-tuple-element.7.s_in, f32[6,16,32,128]{3,2,1,0:T(8,128)S(1)} %get-tuple-element.8.m_in), custom_call_target="tpu_custom_call" | custom-call | tf_op jit(solution)/shard_map/pallas_call | solution.py:460

commit v3 on v2

--- a/solution.py
+++ b/solution.py
@@ -30,7 +30,7 @@
 def kernel(
     elevation, layer_base, stretch, material, buoyancy, lame, shear, relax, weight, velocity, stress, memory,
     v_out, s_out, m_out,
-    sigma, vel, terrain, wide, surf, layers, mat, tables, metric, packs, halo_s, halo_v,
+    sigma, vel, terrain, wide, surf, layers, mat, tables, props, stencil, along, metric, packs, halo_s, halo_v,
     small, local_sem, s_send, s_recv, y_send, y_recv, layer_send, layer_recv, t_send, t_recv, edge_send, edge_recv,
     z_send, z_recv, x_send, x_recv, vy_send, vy_recv, far_sem,
 ):
@@ -50,13 +50,16 @@
         c: pltpu.make_async_copy(stress.at[c], sigma.at[c, 2:18, 8:40, :], local_sem.at[7 + c])
         for c in (0, 3, 4, 1, 2, 5)
     }
-    for c in (0, 3, 4, 1, 2, 5):
+    for c in (0, 3, 4):
+        stress_in[c].start()
+    material_in = pltpu.make_async_copy(material, mat, local_sem.at[15])
+    material_in.start()
+    for c in (1, 2, 5):
         stress_in[c].start()
     elevation_in = pltpu.make_async_copy(elevation, terrain.at[own_slot, 8:40, :], local_sem.at[13])
     velocity_in = pltpu.make_async_copy(velocity, v_out, local_sem.at[14])
-    material_in = pltpu.make_async_copy(material, mat, local_sem.at[15])
     memory_in = pltpu.make_async_copy(memory, m_out, local_sem.at[16])
-    for copy in (elevation_in, material_in, velocity_in, memory_in):
+    for copy in (elevation_in, velocity_in, memory_in):
         copy.start()
 
     barrier = pltpu.get_barrier_semaphore()
@@ -69,11 +72,43 @@
         when(condition, lambda target=target: pl.semaphore_signal(barrier, inc=1, device_id=target, device_id_type=MESH))
     expected = [y_low, y_high & ~before_gap] + [condition for condition, _ in beside]
 
-    for copy in scalars:
-        copy.wait()
-    for k in range(NZ):
-        for row in range(2):
-            layers[row, pl.ds(NZ * z + k, 1), :] = jnp.full((1, NX), small[5 + row, k], jnp.float32)
+    pl.semaphore_wait(barrier, sum(1 if c is None else c.astype(jnp.int32) for c in expected))
+    when(after_gap, lambda: pl.semaphore_signal(far_sem, inc=1, device_id=down_y, device_id_type=MESH))
+
+    def remote(source, to, send, recv, target):
+        return pltpu.make_async_remote_copy(
+            src_ref=source, dst_ref=to, send_sem=send, recv_sem=recv, device_id=target, device_id_type=MESH
+        )
+
+    sends = []
+
+    def send(condition, copy, now=True):
+        sends.append((condition, copy))
+        if now:
+            when(condition, copy.start)
+        return copy
+
+    up_copies = [
+        send(y_high, remote(stress.at[c, :, 30:32, :], sigma.at[c, 2:18, 6:8, :], y_send.at[0, i], y_recv.at[0, i], up_y), now=False)
+        for i, c in enumerate(Y_SENT)
+    ]
+
+    def start_up():
+        for copy in up_copies:
+            copy.start()
+
+    when(y_high & ~before_gap, start_up)
+    for d in range(1, GZ):
+        send(None, remote(elevation, terrain.at[own_slot, 8:40, :], t_send.at[d - 1], t_recv.at[own_slot], {"gz": (z + d) % GZ}))
+    for g in range(GZ):
+        send(x_high & (z == GZ - 1), remote(elevation, terrain.at[0, 8:40, :], t_send.at[3 + g], t_recv.at[0], {"gx": x + 1, "gz": g}))
+        send(x_low & (z == 0), remote(elevation, terrain.at[5, 8:40, :], t_send.at[3 + g], t_recv.at[5], {"gx": x - 1, "gz": g}))
+    for i, c in enumerate(Y_SENT):
+        send(y_low, remote(stress.at[c, :, 0:2, :], sigma.at[c, 2:18, 40:42, :], y_send.at[1, i], y_recv.at[1, i], down_y))
+    send(z_high, remote(stress.at[:, 14:16], sigma.at[:, 0:2, 8:40, :], s_send.at[2], s_recv.at[2], {"gz": z + 1}))
+    send(z_low, remote(stress.at[:, 0:2], sigma.at[:, 18:20, 8:40, :], s_send.at[3], s_recv.at[3], {"gz": z - 1}))
+
+    zero = jnp.zeros((8, NX), jnp.float32)
 
     def pack_spot(k, i):
         at = 4 * (k + (NZ if i == 1 else 0))
@@ -92,57 +127,21 @@
                 pack_layer(held, [sigma[c, 2 + k, 8 + 8 * r : 16 + 8 * r, :] for r in range(4)], i, k, at, spot)
         return tuple(held)
 
+    for copy in scalars:
+        copy.wait()
+    for k in range(NZ):
+        for row in range(2):
+            layers[row, pl.ds(NZ * z + k, 1), :] = jnp.full((1, NX), small[5 + row, k], jnp.float32)
+
     for c in X_PARTS:
         stress_in[c].wait()
-    zero = jnp.zeros((8, NX), jnp.float32)
     held = lax.fori_loop(0, NZ // 2, pack_stress, (zero,) * 8)
     for j in range(8):
         packs[0, j // 4, 8 * (j % 4) : 8 * (j % 4) + 8, :] = held[j]
 
-    pl.semaphore_wait(barrier, sum(1 if c is None else c.astype(jnp.int32) for c in expected))
-    when(after_gap, lambda: pl.semaphore_signal(far_sem, inc=1, device_id=down_y, device_id_type=MESH))
-
-    def remote(source, to, send, recv, target):
-        return pltpu.make_async_remote_copy(
-            src_ref=source, dst_ref=to, send_sem=send, recv_sem=recv, device_id=target, device_id_type=MESH
-        )
-
-    sends = []
-
-    def send(condition, copy, now=True):
-        sends.append((condition, copy))
-        if now:
-            when(condition, copy.start)
-        return copy
-
-    up_copies = [
-        send(y_high, remote(stress.at[c, :, 30:32, :], sigma.at[c, 2:18, 6:8, :], y_send.at[0, i], y_recv.at[0, i], up_y), now=False)
-        for i, c in enumerate(Y_SENT)
-    ]
-
-    def start_up():
-        for copy in up_copies:
-            copy.start()
-
-    when(y_high & ~before_gap, start_up)
-    for d in range(1, GZ):
-        send(None, remote(elevation, terrain.at[own_slot, 8:40, :], t_send.at[d - 1], t_recv.at[own_slot], {"gz": (z + d) % GZ}))
-    for g in range(GZ):
-        send(x_high & (z == GZ - 1), remote(elevation, terrain.at[0, 8:40, :], t_send.at[3 + g], t_recv.at[0], {"gx": x + 1, "gz": g}))
-        send(x_low & (z == 0), remote(elevation, terrain.at[5, 8:40, :], t_send.at[3 + g], t_recv.at[5], {"gx": x - 1, "gz": g}))
     mine = pl.ds(NZ * z, NZ)
     for d in range(1, GZ):
         send(None, remote(layers.at[:, mine, :], layers.at[:, mine, :], layer_send.at[d - 1], layer_recv.at[z], {"gz": (z + d) % GZ}))
-    for i, c in enumerate(Y_SENT):
-        send(y_low, remote(stress.at[c, :, 0:2, :], sigma.at[c, 2:18, 40:42, :], y_send.at[1, i], y_recv.at[1, i], down_y))
-    send(x_high, remote(packs.at[0], halo_s.at[0], s_send.at[0], s_recv.at[0], {"gx": x + 1}))
-    send(x_low, remote(packs.at[0], halo_s.at[1], s_send.at[1], s_recv.at[1], {"gx": x - 1}))
-    send(z_high, remote(stress.at[:, 14:16], sigma.at[:, 0:2, 8:40, :], s_send.at[2], s_recv.at[2], {"gz": z + 1}))
-    send(z_low, remote(stress.at[:, 0:2], sigma.at[:, 18:20, 8:40, :], s_send.at[3], s_recv.at[3], {"gz": z - 1}))
-
-    def arrived(ref, recv):
-        remote(ref, ref, s_send.at[0], recv, {"gz": z}).wait_recv()
-
     columns = []
     for i in range(5):
         column = zero
@@ -155,6 +154,47 @@
     tables[2] = columns[2] * (1.0 / 12.0)
     tables[3] = keep
     tables[4] = (1.0 - keep) * columns[4]
+
+    send(x_high, remote(packs.at[0], halo_s.at[0], s_send.at[0], s_recv.at[0], {"gx": x + 1}))
+    send(x_low, remote(packs.at[0], halo_s.at[1], s_send.at[1], s_recv.at[1], {"gx": x - 1}))
+    material_in.wait()
+
+    def property_layer(k, carry):
+        for r in range(4):
+            rows = slice(8 * r, 8 * r + 8)
+            block_id = mat[k, rows, :]
+            for i in range(5):
+                props[i, k, rows, :] = jnp.take_along_axis(tables[i], block_id, axis=1)
+        return carry
+
+    lax.fori_loop(0, NZ, property_layer, 0)
+
+    offset = lax.broadcasted_iota(jnp.int32, (NX, NX), 0) - lax.broadcasted_iota(jnp.int32, (NX, NX), 1)
+    weights = jnp.zeros((NX, NX), jnp.float32)
+    for distance, factor in ((-2, 1.0), (-1, -8.0), (1, 8.0), (2, -1.0)):
+        weights = jnp.where(offset == distance, factor, weights)
+    stencil[...] = weights.astype(jnp.bfloat16)
+
+    def differentiate_x(parts, field, first, rows, unroll):
+        def layers_of(step, carry):
+            spots = [(i, c, unroll * step + n) for i, c in enumerate(parts) for n in range(unroll)]
+            rest = jnp.concatenate([field[c, k + 2, pl.ds(8 + first, rows), :] for _, c, k in spots], axis=0)
+            total = None
+            for _ in range(3):
+                piece = rest.astype(jnp.bfloat16)
+                rest = rest - piece.astype(jnp.float32)
+                product = jnp.dot(piece, stencil[...], preferred_element_type=jnp.float32)
+                total = product if total is None else total + product
+            for n, (i, _, k) in enumerate(spots):
+                along[i, k, pl.ds(first, rows), :] = total[n * rows : (n + 1) * rows]
+            return carry
+
+        lax.fori_loop(0, NZ // unroll, layers_of, 0)
+
+    differentiate_x(X_PARTS, sigma, 0, NY, 4)
+
+    def arrived(ref, recv):
+        remote(ref, ref, s_send.at[0], recv, {"gz": z}).wait_recv()
 
     def zero_z(first):
         sigma[:, pl.ds(first, 2), 8:40, :] = jnp.zeros((6, 2, NY, NX), jnp.float32)
@@ -254,48 +294,57 @@
     def d_y(field, c, k, first, rows):
         return centred_12(*[field[c, k + 2, pl.ds(8 + first + d, rows), :] for d in (-2, -1, 1, 2)])
 
-    def d_x(field, c, k, first, rows, halo, i):
+    def d_x(c, k, first, rows, halo, i):
         side = lax.broadcasted_iota(jnp.int32, (rows, NX), 1)
-        here = field[c, k + 2, pl.ds(8 + first, rows), :]
         at = 4 * (k + (NZ if i == 1 else 0))
-        beyond = pltpu.roll(halo[0, i // 2, pl.ds(first, rows), :], 126 - at, 1)
-        return centred_12(
-            pltpu.roll(jnp.where(side >= 126, beyond, here), 2, 1), pltpu.roll(jnp.where(side >= 127, beyond, here), 1, 1),
-            pltpu.roll(jnp.where(side < 1, beyond, here), 127, 1), pltpu.roll(jnp.where(side < 2, beyond, here), 126, 1),
-        )
+        fix = pltpu.roll(halo[0, i // 2, pl.ds(first, rows), :], 126 - at, 1)
+        return along[i, k, pl.ds(first, rows), :] + jnp.where((side < 2) | (side >= 126), fix, 0.0)
 
     def join(halo, first, rows):
-        side = lax.broadcasted_iota(jnp.int32, (rows, NX), 1)
+        spot = lax.broadcasted_iota(jnp.int32, (rows, NX), 1) % 4
+        at = pl.ds(first, rows)
         for i in range(2):
-            at = pl.ds(first, rows)
-            halo[0, i, at, :] = jnp.where(side % 4 < 2, halo[0, i, at, :], halo[1, i, at, :])
-
-    def look_up(i, block_id):
-        table = jnp.concatenate([tables[i]] * (block_id.shape[0] // 8), axis=0)
-        return jnp.take_along_axis(table, block_id, axis=1)
+            change = jnp.where(spot < 2, halo[0, i, at, :], halo[1, i, at, :])
+            low = 8.0 * jnp.where(spot == 1, pltpu.roll(change, 127, 1), 0.0) - pltpu.roll(change, 126, 1)
+            high = pltpu.roll(change, 2, 1) - 8.0 * jnp.where(spot == 2, pltpu.roll(change, 1, 1), 0.0)
+            halo[0, i, at, :] = jnp.where(spot < 2, low, high)
 
     def velocity_rows(first, rows, unroll):
         blocks = rows // 8
 
-        def velocity_layer(step, held):
-            held = list(held)
+        def velocity_layer(step, carried):
+            held, last = list(carried[0]), carried[1]
             at = pl.ds(first, rows)
-            for k in [unroll * step + i for i in range(unroll)]:
+            ks = [unroll * step + i for i in range(unroll)]
+            pack_rows(held, [k - unroll for k in ks], last)
+            made = []
+            for k in ks:
                 m_x, m_y, m_z = (metric[i, k, at, :] for i in range(3))
                 grad_k = [d_k(sigma, c, k, first, rows) for c in range(6)]
-                grad_x = [d_x(sigma, c, k, first, rows, halo_s, i) for i, c in enumerate(X_PARTS)]
+                grad_x = [d_x(c, k, first, rows, halo_s, i) for i, c in enumerate(X_PARTS)]
                 grad_y = [d_y(sigma, c, k, first, rows) for c in Y_PARTS]
-                scale = look_up(0, mat[k, at, :])
+                scale = props[0, k, at, :]
+                row = []
                 for c, (a, b, d) in enumerate(((0, 3, 4), (3, 1, 5), (4, 5, 2))):
                     accel = (grad_x[c] - m_x * grad_k[a]) + (grad_y[c] - m_y * grad_k[b]) + m_z * grad_k[d]
                     new = v_out[c, k, at, :] + scale * accel
                     v_out[c, k, at, :] = new
                     vel[c, 2 + k, pl.ds(8 + first, rows), :] = new
+                    row.append(new)
+                made.append(row)
+            return tuple(held), made
+
+        def pack_rows(held, ks, made):
+            for k, row in zip(ks, made):
+                for c in range(3):
                     spot_at, spot = pack_spot(k, c)
-                    pack_layer(held, [new[8 * r : 8 * r + 8] for r in range(blocks)], c, k, spot_at, spot)
-            return tuple(held)
-
-        held = lax.fori_loop(0, NZ // unroll, velocity_layer, (zero,) * (2 * blocks))
+                    pack_layer(held, [row[c][8 * r : 8 * r + 8] for r in range(blocks)], c, k, spot_at, spot)
+
+        nothing = jnp.zeros((rows, NX), jnp.float32)
+        start = ((zero,) * (2 * blocks), [[nothing] * 3 for _ in range(unroll)])
+        held, last = lax.fori_loop(0, NZ // unroll, velocity_layer, start)
+        held = list(held)
+        pack_rows(held, range(NZ - unroll, NZ), last)
         for j in range(2 * blocks):
             packs[1, j // blocks, pl.ds(first + 8 * (j % blocks), 8), :] = held[j]
 
@@ -331,7 +380,7 @@
         start_up()
 
     when(before_gap, start_far)
-    for copy in (stress_in[1], stress_in[2], stress_in[5], velocity_in, material_in):
+    for copy in (stress_in[1], stress_in[2], stress_in[5], velocity_in):
         copy.wait()
     when(x_low, lambda: arrived(halo_s.at[0], s_recv.at[0]))
     when(x_high, lambda: arrived(halo_s.at[1], s_recv.at[1]))
@@ -363,63 +412,59 @@
         when(low & y_low, low_copy.start)
         when(~low & y_high, high_copy.start)
         send_rows(part, first, 8)
+        if part == 1:
+            differentiate_x(range(3), vel, 8, 16, 4)
+        differentiate_x(range(3), vel, first, 8, 8)
 
     memory_in.wait()
 
-    def stress_rows(first, rows, ks):
+    def stress_rows(first, rows, unroll, steps, stride=1):
         at = pl.ds(first, rows)
-        for k in ks:
-            m_x, m_y, m_z = (metric[i, k, at, :] for i in range(3))
-            along_k = [d_k(vel, c, k, first, rows) for c in range(3)]
-            along_x = [d_x(vel, c, k, first, rows, halo_v, c) - m_x * along_k[c] for c in range(3)]
-            along_y = [d_y(vel, c, k, first, rows) - m_y * along_k[c] for c in range(3)]
-            along_z = [m_z * along_k[c] for c in range(3)]
-            block_id = mat[k, at, :]
-            lam, mu, kept, gain = (look_up(i, block_id) for i in range(1, 5))
-            volume = lam * (along_x[0] + along_y[1] + along_z[2])
-            twice = mu + mu
-            rates = (
-                volume + twice * along_x[0],
-                volume + twice * along_y[1],
-                volume + twice * along_z[2],
-                mu * (along_y[0] + along_x[1]),
-                mu * (along_z[0] + along_x[2]),
-                mu * (along_z[1] + along_y[2]),
-            )
-            for c, rate in enumerate(rates):
-                new = kept * m_out[c, k, at, :] + gain * rate
-                m_out[c, k, at, :] = new
-                s_out[c, k, at, :] = sigma[c, 2 + k, pl.ds(8 + first, rows), :] + STEP * (rate - new)
-
-    def inner(step, carry):
-        stress_rows(8, 16, (2 * step, 2 * step + 1))
-        return carry
+
+        def stress_layer(step, carry):
+            for k in [unroll * stride * step + i for i in range(unroll)]:
+                grad_x = [d_x(c, k, first, rows, halo_v, c) for c in range(3)]
+                m_x, m_y, m_z = (metric[i, k, at, :] for i in range(3))
+                along_k = [d_k(vel, c, k, first, rows) for c in range(3)]
+                along_x = [grad_x[c] - m_x * along_k[c] for c in range(3)]
+                along_y = [d_y(vel, c, k, first, rows) - m_y * along_k[c] for c in range(3)]
+                along_z = [m_z * along_k[c] for c in range(3)]
+                lam, mu, kept, gain = (props[i, k, at, :] for i in range(1, 5))
+                volume = lam * (along_x[0] + along_y[1] + along_z[2])
+                twice = mu + mu
+                rates = (
+                    volume + twice * along_x[0],
+                    volume + twice * along_y[1],
+                    volume + twice * along_z[2],
+                    mu * (along_y[0] + along_x[1]),
+                    mu * (along_z[0] + along_x[2]),
+                    mu * (along_z[1] + along_y[2]),
+                )
+                for c, rate in enumerate(rates):
+                    new = kept * m_out[c, k, at, :] + gain * rate
+                    m_out[c, k, at, :] = new
+                    s_out[c, k, at, :] = sigma[c, 2 + k, pl.ds(8 + first, rows), :] + STEP * (rate - new)
+            return carry
+
+        lax.fori_loop(steps[0], steps[1], stress_layer, 0)
 
     wait_x(0, 8, 16)
-    lax.fori_loop(1, NZ // 2 - 1, inner, 0)
+    stress_rows(8, 16, 2, (1, NZ // 2 - 1))
     wait_z(0, 8, 16)
-    lax.fori_loop(0, 2, lambda step, carry: inner(step * (NZ // 2 - 1), carry), 0)
+    stress_rows(8, 16, 2, (0, 2), NZ // 2 - 1)
     for part, low, first, outer in strips:
         wait_x(part, first, 8)
         wait_z(part, first, 8)
         when(low & y_low, lambda: arrived(vel.at[:, 2:18, 6:8, :], vy_recv.at[0]))
         when(~low & y_high, lambda: arrived(vel.at[:, 2:18, 40:42, :], vy_recv.at[1]))
-
-        def strip(step, carry):
-            stress_rows(first, 8, [4 * step + i for i in range(4)])
-            return carry
-
-        lax.fori_loop(0, NZ // 4, strip, 0)
+        stress_rows(first, 8, 4, (0, NZ // 4))
     for condition, copy in sends:
         when(condition, copy.wait_send)
 
 
 def write_out(v_in, s_in, m_in, v_ref, s_ref, m_ref, sems):
-    copies = [pltpu.make_async_copy(v_in, v_ref, sems.at[0])]
-    for half in range(2):
-        rows = slice(3 * half, 3 * half + 3)
-        copies.append(pltpu.make_async_copy(s_in.at[rows], s_ref.at[rows], sems.at[1 + half]))
-        copies.append(pltpu.make_async_copy(m_in.at[rows], m_ref.at[rows], sems.at[3 + half]))
+    pairs = [(v_in, v_ref, c) for c in range(3)] + [(a, b, c) for a, b in ((s_in, s_ref), (m_in, m_ref)) for c in range(6)]
+    copies = [pltpu.make_async_copy(a.at[c], b.at[c], sems.at[i]) for i, (a, b, c) in enumerate(pairs)]
     for copy in copies:
         copy.start()
     for copy in copies:
@@ -444,6 +489,9 @@
             vmem((2, GZ * NZ, NX), f32),
             vmem((NZ, NY, NX), jnp.int32),
             vmem((5, 8, NX), f32),
+            vmem((5, NZ, NY, NX), f32),
+            vmem((NX, NX), jnp.bfloat16),
+            vmem((3, NZ, NY, NX), f32),
             vmem((3, NZ, NY, NX), f32),
             vmem((2, 2, NY, NX), f32),
             vmem((2, 2, NY, NX), f32),
@@ -462,7 +510,7 @@
         out_shape=tuple(jax.ShapeDtypeStruct(shape, f32) for shape in outputs),
         in_specs=[pl.BlockSpec(memory_space=vmem)] * 3,
         out_specs=tuple(pl.BlockSpec(memory_space=pltpu.HBM) for _ in outputs),
-        scratch_shapes=[dma((5,))],
+        scratch_shapes=[dma((15,))],
         compiler_params=pltpu.CompilerParams(vmem_limit_bytes=8 << 20),
     )(*results)
 

time: 29.7 us -> 28.9 us (0.973)
  the two profiles are of different devices: /device:TPU:15 before, /device:TPU:7 now
where the time goes in v3:
time: 28.9 us; the launch traced here: 28.8 us
  Pallas kernels  28.2 us (98%)
  between operations  0.64 us (2%)
    pallas_call x1, Pallas kernels, local(): pl.pallas_call(kernel, out_shape=tuple((vmem(shape, f32) for shape in out...  26.2 us
    pallas_call x1, Pallas kernels, local(): pl.pallas_call(write_out, out_shape=tuple((jax.ShapeDtypeStruct(shape, f3...  2.04 us

profile of v3, /device:TPU:7, one launch (start us, length us, event | category | flops | bytes accessed | tf_op | source)
XLA Modules:
  0.0 28.8 jit_solution(15759161936495699191)
XLA Ops:
  0.6 26.2 %shard_map.139 = (f32[3,16,32,128]{3,2,1,0:T(8,128)S(1)}, f32[6,16,32,128]{3,2,1,0:T(8,128)S(1)}, f32[6,16,32,128]{3,2,1,0:T(8,128)S(1)}) custom-call(s32[32,32]{1,0:T(8,128)} %elevation.1, f32[16]{0:T(128)} %layer_base.1, f32[16]{0:T(128)} %stretch.1, s32[16,32,128]{2,1,0:T(8,128)} %material.1, f32[16]{0:T(128)} %buoyancy.1, f32[16]{0:T(128)} %lame.1, ...), custom_call_target="tpu_custom_call" | custom-call | tf_op jit(solution)/shard_map/pallas_call | solution.py:478
  26.8 2.0 %shard_map.140 = (f32[3,16,32,128]{3,2,1,0:T(8,128)}, f32[6,16,32,128]{3,2,1,0:T(8,128)}, f32[6,16,32,128]{3,2,1,0:T(8,128)}) custom-call(f32[3,16,32,128]{3,2,1,0:T(8,128)S(1)} %get-tuple-element.6.v_in, f32[6,16,32,128]{3,2,1,0:T(8,128)S(1)} %get-tuple-element.7.s_in, f32[6,16,32,128]{3,2,1,0:T(8,128)S(1)} %get-tuple-element.8.m_in), custom_call_target="tpu_custom_call" | custom-call | tf_op jit(solution)/shard_map/pallas_call | solution.py:508

commit v4 on v3

--- a/solution.py
+++ b/solution.py
@@ -32,7 +32,7 @@
     v_out, s_out, m_out,
     sigma, vel, terrain, wide, surf, layers, mat, tables, props, stencil, along, metric, packs, halo_s, halo_v,
     small, local_sem, s_send, s_recv, y_send, y_recv, layer_send, layer_recv, t_send, t_recv, edge_send, edge_recv,
-    z_send, z_recv, x_send, x_recv, vy_send, vy_recv, far_sem,
+    z_send, z_recv, x_send, x_recv, vy_send, vy_recv, zs_send, zs_recv, gap_out, gap_in, gap_sem, far_sem,
 ):
     x, y, z = lax.axis_index("gx"), lax.axis_index("gy"), lax.axis_index("gz")
     x_low, x_high = x > 0, x < GX - 1
@@ -105,8 +105,29 @@
         send(x_low & (z == 0), remote(elevation, terrain.at[5, 8:40, :], t_send.at[3 + g], t_recv.at[5], {"gx": x - 1, "gz": g}))
     for i, c in enumerate(Y_SENT):
         send(y_low, remote(stress.at[c, :, 0:2, :], sigma.at[c, 2:18, 40:42, :], y_send.at[1, i], y_recv.at[1, i], down_y))
-    send(z_high, remote(stress.at[:, 14:16], sigma.at[:, 0:2, 8:40, :], s_send.at[2], s_recv.at[2], {"gz": z + 1}))
-    send(z_low, remote(stress.at[:, 0:2], sigma.at[:, 18:20, 8:40, :], s_send.at[3], s_recv.at[3], {"gz": z - 1}))
+    odd = y % 2
+    strips = []
+    for part in (1, 2):
+        low = (odd == 1) if part == 1 else (odd == 0)
+        side = odd if part == 1 else 1 - odd
+        strips.append((part, low, pl.multiple_of(24 - 24 * side, 8), pl.multiple_of(40 - 40 * side, 8)))
+    z_parts = [(0, 8, 16)] + [(part, first, 8) for part, _, first, _ in strips]
+    z_copies = []
+    for part, first, rows in z_parts:
+        at, to = pl.ds(first, rows), pl.ds(8 + first, rows)
+        z_copies.append((
+            send(z_high, remote(stress.at[:, 14:16, at, :], sigma.at[:, 0:2, to, :], zs_send.at[0, part], zs_recv.at[0, part], {"gz": z + 1}), now=False),
+            send(z_low, remote(stress.at[:, 0:2, at, :], sigma.at[:, 18:20, to, :], zs_send.at[1, part], zs_recv.at[1, part], {"gz": z - 1}), now=False),
+        ))
+
+    def start_z(part, condition):
+        when(z_high if condition is None else condition & z_high, z_copies[part][0].start)
+        when(z_low if condition is None else condition & z_low, z_copies[part][1].start)
+
+    start_z(2, after_gap)
+    start_z(0, None)
+    start_z(1, None)
+    start_z(2, ~after_gap)
 
     zero = jnp.zeros((8, NX), jnp.float32)
 
@@ -385,20 +406,64 @@
     when(x_low, lambda: arrived(halo_s.at[0], s_recv.at[0]))
     when(x_high, lambda: arrived(halo_s.at[1], s_recv.at[1]))
     join(halo_s, 0, NY)
-    when(z_low, lambda: arrived(sigma.at[:, 0:2, 8:40, :], s_recv.at[2]))
-    when(z_high, lambda: arrived(sigma.at[:, 18:20, 8:40, :], s_recv.at[3]))
+    def wait_stress_z(part, condition):
+        _, first, rows = z_parts[part]
+        to = pl.ds(8 + first, rows)
+        when(condition & z_low, lambda: arrived(sigma.at[:, 0:2, to, :], zs_recv.at[0, part]))
+        when(condition & z_high, lambda: arrived(sigma.at[:, 18:20, to, :], zs_recv.at[1, part]))
+
+    gap_copy = remote(gap_out, gap_in, gap_sem.at[0], gap_sem.at[1], down_y)
+    sends.append((after_gap, gap_copy))
+
+    def gap_package():
+        top = lax.broadcasted_iota(jnp.int32, (8, NX), 0) == 0
+
+        def layers_of(step, carry):
+            for k in (2 * step, 2 * step + 1):
+                scale = props[0, k, 0:8, :]
+                for c in range(6):
+                    gap_out[3 + c, k] = (scale * d_k(sigma, c, k, 0, 8))[0:2]
+                gap_out[9, k] = scale[0:2]
+                for i, (c_x, c_y) in enumerate(zip(X_PARTS, Y_PARTS)):
+                    here, after_1, after_2 = (sigma[c_y, k + 2, 8 + d : 16 + d, :] for d in range(3))
+                    before_1 = jnp.where(top, 0.0, pltpu.roll(here, 1, 0))
+                    grad_y = 8.0 * (after_1 - before_1) - after_2
+                    known = v_out[i, k, 0:8, :] + scale * (d_x(c_x, k, 0, 8, halo_s, i) + grad_y)
+                    gap_out[i, k] = known[0:2]
+            return carry
+
+        lax.fori_loop(0, NZ // 2, layers_of, 0)
+        gap_copy.start()
+
+    def gap_velocity():
+        arrived(gap_in, gap_sem.at[1])
+
+        def layers_of(step, carry):
+            for k in (2 * step, 2 * step + 1):
+                m_x, m_y, m_z = (metric[i, k, NY : NY + 2, :] for i in range(3))
+                for i, (a, b, d) in enumerate(((0, 3, 4), (3, 1, 5), (4, 5, 2))):
+                    edge = sigma[Y_PARTS[i], k + 2, 38:40, :]
+                    beyond = jnp.concatenate([edge[0:1] - 8.0 * edge[1:2], edge[1:2]], axis=0)
+                    known = gap_in[i, k] + gap_in[9, k] * beyond
+                    vel[i, 2 + k, 40:42, :] = known - m_x * gap_in[3 + a, k] - m_y * gap_in[3 + b, k] + m_z * gap_in[3 + d, k]
+            return carry
+
+        lax.fori_loop(0, NZ // 2, layers_of, 0)
+
+    def gap_metrics():
+        for part in range(3):
+            wide[part, 48:64, :] = jnp.zeros((16, NX), jnp.float32)
+        metrics(NY, 8)
+
+    wait_stress_z(2, after_gap)
+    when(after_gap, gap_package)
+    wait_stress_z(0, z >= 0)
     velocity_rows(8, 16, 2)
     send_rows(0, 8, 16)
 
-    odd = y % 2
-    strips = []
-    for part in (1, 2):
-        low = (odd == 1) if part == 1 else (odd == 0)
-        side = odd if part == 1 else 1 - odd
-        strips.append((part, low, pl.multiple_of(24 - 24 * side, 8), pl.multiple_of(40 - 40 * side, 8)))
     low_copy = remote(vel.at[:, 2:18, 8:10, :], vel.at[:, 2:18, 40:42, :], vy_send.at[1], vy_recv.at[1], down_y)
     high_copy = remote(vel.at[:, 2:18, 38:40, :], vel.at[:, 2:18, 6:8, :], vy_send.at[0], vy_recv.at[0], up_y)
-    sends.append((y_low, low_copy))
+    sends.append((y_low & ~after_gap, low_copy))
     sends.append((y_high, high_copy))
     for part, low, first, outer in strips:
         when(low & y_low, lambda: arrived(terrain.at[:, 0:8, :], edge_recv.at[0]))
@@ -408,13 +473,15 @@
         for i, c in enumerate(Y_SENT):
             when(low & y_low, lambda: arrived(sigma.at[c, 2:18, 6:8, :], y_recv.at[0, i]))
             when(~low & y_high, lambda: arrived(sigma.at[c, 2:18, 40:42, :], y_recv.at[1, i]))
+        wait_stress_z(part, (z >= 0) if part == 1 else ~after_gap)
         velocity_rows(first, 8, 4)
-        when(low & y_low, low_copy.start)
+        when(low & y_low & ~after_gap, low_copy.start)
         when(~low & y_high, high_copy.start)
         send_rows(part, first, 8)
         if part == 1:
             differentiate_x(range(3), vel, 8, 16, 4)
         differentiate_x(range(3), vel, first, 8, 8)
+    when(before_gap, gap_metrics)
 
     memory_in.wait()
 
@@ -456,7 +523,9 @@
         wait_x(part, first, 8)
         wait_z(part, first, 8)
         when(low & y_low, lambda: arrived(vel.at[:, 2:18, 6:8, :], vy_recv.at[0]))
-        when(~low & y_high, lambda: arrived(vel.at[:, 2:18, 40:42, :], vy_recv.at[1]))
+        when(~low & y_high & ~before_gap, lambda: arrived(vel.at[:, 2:18, 40:42, :], vy_recv.at[1]))
+        if part == 2:
+            when(before_gap, gap_velocity)
         stress_rows(first, 8, 4, (0, NZ // 4))
     for condition, copy in sends:
         when(condition, copy.wait_send)
@@ -484,7 +553,7 @@
             vmem((6, 20, 48, NX), f32),
             vmem((3, 20, 48, NX), f32),
             vmem((6, 48, 32), jnp.int32),
-            vmem((3, 48, NX), f32),
+            vmem((3, 64, NX), f32),
             vmem((3, 24, NX), f32),
             vmem((2, GZ * NZ, NX), f32),
             vmem((NZ, NY, NX), jnp.int32),
@@ -492,13 +561,17 @@
             vmem((5, NZ, NY, NX), f32),
             vmem((NX, NX), jnp.bfloat16),
             vmem((3, NZ, NY, NX), f32),
-            vmem((3, NZ, NY, NX), f32),
+            vmem((3, NZ, NY + 8, NX), f32),
             vmem((2, 2, NY, NX), f32),
             vmem((2, 2, NY, NX), f32),
             vmem((2, 2, NY, NX), f32),
             pltpu.SMEM((7, 16), f32),
             dma((17,)), dma((4,)), dma((4,)), dma((2, 3)), dma((2, 3)), dma((3,)), dma((4,)), dma((7,)), dma((6,)), dma((2,)), dma((2,)),
             dma((2, 3)), dma((2, 3)), dma((2, 3)), dma((2, 3)), dma((2,)), dma((2,)),
+            dma((2, 3)), dma((2, 3)),
+            vmem((10, NZ, 2, NX), f32),
+            vmem((10, NZ, 2, NX), f32),
+            dma((2,)),
             pltpu.SemaphoreType.REGULAR,
         ],
         compiler_params=pltpu.CompilerParams(

time: 28.9 us -> 28.4 us (0.983)
  the two profiles are of different devices: /device:TPU:7 before, /device:TPU:39 now
where the time goes in v4:
time: 28.4 us; the launch traced here: 28.3 us
  Pallas kernels  27.6 us (97%)
  between operations  0.64 us (2%)
    pallas_call x1, Pallas kernels, local(): pl.pallas_call(kernel, out_shape=tuple((vmem(shape, f32) for shape in out...  25.6 us
    pallas_call x1, Pallas kernels, local(): pl.pallas_call(write_out, out_shape=tuple((jax.ShapeDtypeStruct(shape, f3...  2.04 us

profile of v4, /device:TPU:39, one launch (start us, length us, event | category | flops | bytes accessed | tf_op | source)
XLA Modules:
  0.0 28.3 jit_solution(14027755954750942421)
XLA Ops:
  0.6 25.6 %shard_map.139 = (f32[3,16,32,128]{3,2,1,0:T(8,128)S(1)}, f32[6,16,32,128]{3,2,1,0:T(8,128)S(1)}, f32[6,16,32,128]{3,2,1,0:T(8,128)S(1)}) custom-call(s32[32,32]{1,0:T(8,128)} %elevation.1, f32[16]{0:T(128)} %layer_base.1, f32[16]{0:T(128)} %stretch.1, s32[16,32,128]{2,1,0:T(8,128)} %material.1, f32[16]{0:T(128)} %buoyancy.1, f32[16]{0:T(128)} %lame.1, ...), custom_call_target="tpu_custom_call" | custom-call | tf_op jit(solution)/shard_map/pallas_call | solution.py:547
  26.2 2.0 %shard_map.140 = (f32[3,16,32,128]{3,2,1,0:T(8,128)}, f32[6,16,32,128]{3,2,1,0:T(8,128)}, f32[6,16,32,128]{3,2,1,0:T(8,128)}) custom-call(f32[3,16,32,128]{3,2,1,0:T(8,128)S(1)} %get-tuple-element.6.v_in, f32[6,16,32,128]{3,2,1,0:T(8,128)S(1)} %get-tuple-element.7.s_in, f32[6,16,32,128]{3,2,1,0:T(8,128)S(1)} %get-tuple-element.8.m_in), custom_call_target="tpu_custom_call" | custom-call | tf_op jit(solution)/shard_map/pallas_call | solution.py:581

commit v5 on v4

--- a/solution.py
+++ b/solution.py
@@ -88,21 +88,21 @@
             when(condition, copy.start)
         return copy
 
-    up_copies = [
-        send(y_high, remote(stress.at[c, :, 30:32, :], sigma.at[c, 2:18, 6:8, :], y_send.at[0, i], y_recv.at[0, i], up_y), now=False)
-        for i, c in enumerate(Y_SENT)
-    ]
-
-    def start_up():
-        for copy in up_copies:
-            copy.start()
-
-    when(y_high & ~before_gap, start_up)
     for d in range(1, GZ):
         send(None, remote(elevation, terrain.at[own_slot, 8:40, :], t_send.at[d - 1], t_recv.at[own_slot], {"gz": (z + d) % GZ}))
     for g in range(GZ):
         send(x_high & (z == GZ - 1), remote(elevation, terrain.at[0, 8:40, :], t_send.at[3 + g], t_recv.at[0], {"gx": x + 1, "gz": g}))
         send(x_low & (z == 0), remote(elevation, terrain.at[5, 8:40, :], t_send.at[3 + g], t_recv.at[5], {"gx": x - 1, "gz": g}))
+    up_copies = [
+        send(y_high, remote(stress.at[c, :, 30:32, :], sigma.at[c, 2:18, 6:8, :], y_send.at[0, i], y_recv.at[0, i], up_y), now=False)
+        for i, c in enumerate(Y_SENT)
+    ]
+
+    def start_up():
+        for copy in up_copies:
+            copy.start()
+
+    when(y_high & ~before_gap, start_up)
     for i, c in enumerate(Y_SENT):
         send(y_low, remote(stress.at[c, :, 0:2, :], sigma.at[c, 2:18, 40:42, :], y_send.at[1, i], y_recv.at[1, i], down_y))
     odd = y % 2
@@ -400,7 +400,6 @@
         edge_up.start()
         start_up()
 
-    when(before_gap, start_far)
     for copy in (stress_in[1], stress_in[2], stress_in[5], velocity_in):
         copy.wait()
     when(x_low, lambda: arrived(halo_s.at[0], s_recv.at[0]))
@@ -460,6 +459,8 @@
     wait_stress_z(0, z >= 0)
     velocity_rows(8, 16, 2)
     send_rows(0, 8, 16)
+    differentiate_x(range(3), vel, 8, 16, 4)
+    when(before_gap, start_far)
 
     low_copy = remote(vel.at[:, 2:18, 8:10, :], vel.at[:, 2:18, 40:42, :], vy_send.at[1], vy_recv.at[1], down_y)
     high_copy = remote(vel.at[:, 2:18, 38:40, :], vel.at[:, 2:18, 6:8, :], vy_send.at[0], vy_recv.at[0], up_y)
@@ -478,8 +479,7 @@
         when(low & y_low & ~after_gap, low_copy.start)
         when(~low & y_high, high_copy.start)
         send_rows(part, first, 8)
-        if part == 1:
-            differentiate_x(range(3), vel, 8, 16, 4)
+    for _, _, first, _ in strips:
         differentiate_x(range(3), vel, first, 8, 8)
     when(before_gap, gap_metrics)
 

time: 28.4 us -> 28.4 us (level)
  no operation moved by 1% of the time
where the time goes in v5:
time: 28.4 us
  Pallas kernels  27.7 us (98%)
  between operations  0.64 us (2%)
    pallas_call x1, Pallas kernels, local(): pl.pallas_call(kernel, out_shape=tuple((vmem(shape, f32) for shape in out...  25.7 us
    pallas_call x1, Pallas kernels, local(): pl.pallas_call(write_out, out_shape=tuple((jax.ShapeDtypeStruct(shape, f3...  2.04 us

profile of v5, /device:TPU:39, one launch (start us, length us, event | category | flops | bytes accessed | tf_op | source)
XLA Modules:
  0.0 28.4 jit_solution(8916992528010830433)
XLA Ops:
  0.6 25.7 %shard_map.139 = (f32[3,16,32,128]{3,2,1,0:T(8,128)S(1)}, f32[6,16,32,128]{3,2,1,0:T(8,128)S(1)}, f32[6,16,32,128]{3,2,1,0:T(8,128)S(1)}) custom-call(s32[32,32]{1,0:T(8,128)} %elevation.1, f32[16]{0:T(128)} %layer_base.1, f32[16]{0:T(128)} %stretch.1, s32[16,32,128]{2,1,0:T(8,128)} %material.1, f32[16]{0:T(128)} %buoyancy.1, f32[16]{0:T(128)} %lame.1, ...), custom_call_target="tpu_custom_call" | custom-call | tf_op jit(solution)/shard_map/pallas_call | solution.py:547
  26.3 2.0 %shard_map.140 = (f32[3,16,32,128]{3,2,1,0:T(8,128)}, f32[6,16,32,128]{3,2,1,0:T(8,128)}, f32[6,16,32,128]{3,2,1,0:T(8,128)}) custom-call(f32[3,16,32,128]{3,2,1,0:T(8,128)S(1)} %get-tuple-element.6.v_in, f32[6,16,32,128]{3,2,1,0:T(8,128)S(1)} %get-tuple-element.7.s_in, f32[6,16,32,128]{3,2,1,0:T(8,128)S(1)} %get-tuple-element.8.m_in), custom_call_target="tpu_custom_call" | custom-call | tf_op jit(solution)/shard_map/pallas_call | solution.py:581

commit v6 on v5

--- a/solution.py
+++ b/solution.py
@@ -32,13 +32,14 @@
     v_out, s_out, m_out,
     sigma, vel, terrain, wide, surf, layers, mat, tables, props, stencil, along, metric, packs, halo_s, halo_v,
     small, local_sem, s_send, s_recv, y_send, y_recv, layer_send, layer_recv, t_send, t_recv, edge_send, edge_recv,
-    z_send, z_recv, x_send, x_recv, vy_send, vy_recv, zs_send, zs_recv, gap_out, gap_in, gap_sem, far_sem,
+    z_send, z_recv, x_send, x_recv, vy_send, vy_recv, zs_send, zs_recv, gap_out, gap_in, gap_sem, pass_send, pass_recv, far_sem,
 ):
     x, y, z = lax.axis_index("gx"), lax.axis_index("gy"), lax.axis_index("gz")
     x_low, x_high = x > 0, x < GX - 1
     y_low, y_high = y > 0, y < GY - 1
     z_low, z_high = z > 0, z < GZ - 1
     before_gap, after_gap = y == GY // 2 - 1, y == GY // 2
+    at_gap = before_gap | after_gap
     lane = lax.broadcasted_iota(jnp.int32, (8, NX), 1)
 
     own_slot = 1 + z
@@ -93,6 +94,8 @@
     for g in range(GZ):
         send(x_high & (z == GZ - 1), remote(elevation, terrain.at[0, 8:40, :], t_send.at[3 + g], t_recv.at[0], {"gx": x + 1, "gz": g}))
         send(x_low & (z == 0), remote(elevation, terrain.at[5, 8:40, :], t_send.at[3 + g], t_recv.at[5], {"gx": x - 1, "gz": g}))
+    gap_terrain = terrain.at[own_slot, 40:48, :]
+    send(after_gap, remote(elevation.at[0:8, :], gap_terrain, gap_sem.at[2], gap_sem.at[3], down_y))
     up_copies = [
         send(y_high, remote(stress.at[c, :, 30:32, :], sigma.at[c, 2:18, 6:8, :], y_send.at[0, i], y_recv.at[0, i], up_y), now=False)
         for i, c in enumerate(Y_SENT)
@@ -238,12 +241,75 @@
         halo_v[side] = jnp.zeros((2, NY, NX), jnp.float32)
         terrain[slot, 8:40, :] = jnp.zeros((32, 32), jnp.int32)
 
+        def zero_top():
+            terrain[slot, 40:48, :] = jnp.zeros((8, 32), jnp.int32)
+
+        when(before_gap, zero_top)
+
     when(z == 0, lambda: zero_z(0))
     when(z == GZ - 1, lambda: zero_z(18))
     when(y == 0, lambda: zero_y(0))
     when(y == GY - 1, lambda: zero_y(40))
     when(x == 0, lambda: zero_x(0, 0))
     when(x == GX - 1, lambda: zero_x(1, 5))
+
+    def d_k(field, c, k, first, rows):
+        return centred_12(*[field[c, k + 2 + d, pl.ds(8 + first, rows), :] for d in (-2, -1, 1, 2)])
+
+    def d_y(field, c, k, first, rows):
+        return centred_12(*[field[c, k + 2, pl.ds(8 + first + d, rows), :] for d in (-2, -1, 1, 2)])
+
+    def d_x(c, k, first, rows, halo, i):
+        side = lax.broadcasted_iota(jnp.int32, (rows, NX), 1)
+        at = 4 * (k + (NZ if i == 1 else 0))
+        fix = pltpu.roll(halo[0, i // 2, pl.ds(first, rows), :], 126 - at, 1)
+        return along[i, k, pl.ds(first, rows), :] + jnp.where((side < 2) | (side >= 126), fix, 0.0)
+
+    def join(halo, first, rows):
+        spot = lax.broadcasted_iota(jnp.int32, (rows, NX), 1) % 4
+        at = pl.ds(first, rows)
+        for i in range(2):
+            change = jnp.where(spot < 2, halo[0, i, at, :], halo[1, i, at, :])
+            low = 8.0 * jnp.where(spot == 1, pltpu.roll(change, 127, 1), 0.0) - pltpu.roll(change, 126, 1)
+            high = pltpu.roll(change, 2, 1) - 8.0 * jnp.where(spot == 2, pltpu.roll(change, 1, 1), 0.0)
+            halo[0, i, at, :] = jnp.where(spot < 2, low, high)
+
+    for copy in (stress_in[1], stress_in[2], stress_in[5], velocity_in):
+        copy.wait()
+    when(x_low, lambda: arrived(halo_s.at[0], s_recv.at[0]))
+    when(x_high, lambda: arrived(halo_s.at[1], s_recv.at[1]))
+    join(halo_s, 0, NY)
+    def wait_stress_z(part, condition):
+        _, first, rows = z_parts[part]
+        to = pl.ds(8 + first, rows)
+        when(condition & z_low, lambda: arrived(sigma.at[:, 0:2, to, :], zs_recv.at[0, part]))
+        when(condition & z_high, lambda: arrived(sigma.at[:, 18:20, to, :], zs_recv.at[1, part]))
+
+    gap_copy = remote(gap_out, gap_in, gap_sem.at[0], gap_sem.at[1], down_y)
+    sends.append((after_gap, gap_copy))
+
+    def gap_package():
+        top = lax.broadcasted_iota(jnp.int32, (8, NX), 0) == 0
+
+        def layers_of(step, carry):
+            for k in (2 * step, 2 * step + 1):
+                scale = props[0, k, 0:8, :]
+                for c in range(6):
+                    gap_out[3 + c, k] = (scale * d_k(sigma, c, k, 0, 8))[0:2]
+                gap_out[9, k] = scale[0:2]
+                for i, (c_x, c_y) in enumerate(zip(X_PARTS, Y_PARTS)):
+                    here, after_1, after_2 = (sigma[c_y, k + 2, 8 + d : 16 + d, :] for d in range(3))
+                    before_1 = jnp.where(top, 0.0, pltpu.roll(here, 1, 0))
+                    grad_y = 8.0 * (after_1 - before_1) - after_2
+                    known = v_out[i, k, 0:8, :] + scale * (d_x(c_x, k, 0, 8, halo_s, i) + grad_y)
+                    gap_out[i, k] = known[0:2]
+            return carry
+
+        lax.fori_loop(0, NZ // 2, layers_of, 0)
+        gap_copy.start()
+
+    wait_stress_z(2, after_gap)
+    when(after_gap, gap_package)
 
     elevation_in.wait()
     for d in range(1, GZ):
@@ -253,7 +319,7 @@
     when(x_high, lambda: arrived(terrain.at[5, 8:40, :], t_recv.at[5]))
     edge_up = send(y_high, remote(terrain.at[:, 32:40, :], terrain.at[:, 0:8, :], edge_send.at[0], edge_recv.at[0], up_y), now=False)
     when(y_high & ~before_gap, edge_up.start)
-    send(y_low, remote(terrain.at[:, 8:16, :], terrain.at[:, 40:48, :], edge_send.at[1], edge_recv.at[1], down_y))
+    send(y_low & ~after_gap, remote(terrain.at[:, 8:16, :], terrain.at[:, 40:48, :], edge_send.at[1], edge_recv.at[1], down_y))
 
     def heights(row):
         rows = pl.ds(row, 8)
@@ -308,27 +374,6 @@
             return total
 
         lax.fori_loop(0, NZ // 4, layer, upper)
-
-    def d_k(field, c, k, first, rows):
-        return centred_12(*[field[c, k + 2 + d, pl.ds(8 + first, rows), :] for d in (-2, -1, 1, 2)])
-
-    def d_y(field, c, k, first, rows):
-        return centred_12(*[field[c, k + 2, pl.ds(8 + first + d, rows), :] for d in (-2, -1, 1, 2)])
-
-    def d_x(c, k, first, rows, halo, i):
-        side = lax.broadcasted_iota(jnp.int32, (rows, NX), 1)
-        at = 4 * (k + (NZ if i == 1 else 0))
-        fix = pltpu.roll(halo[0, i // 2, pl.ds(first, rows), :], 126 - at, 1)
-        return along[i, k, pl.ds(first, rows), :] + jnp.where((side < 2) | (side >= 126), fix, 0.0)
-
-    def join(halo, first, rows):
-        spot = lax.broadcasted_iota(jnp.int32, (rows, NX), 1) % 4
-        at = pl.ds(first, rows)
-        for i in range(2):
-            change = jnp.where(spot < 2, halo[0, i, at, :], halo[1, i, at, :])
-            low = 8.0 * jnp.where(spot == 1, pltpu.roll(change, 127, 1), 0.0) - pltpu.roll(change, 126, 1)
-            high = pltpu.roll(change, 2, 1) - 8.0 * jnp.where(spot == 2, pltpu.roll(change, 1, 1), 0.0)
-            halo[0, i, at, :] = jnp.where(spot < 2, low, high)
 
     def velocity_rows(first, rows, unroll):
         blocks = rows // 8
@@ -400,40 +445,6 @@
         edge_up.start()
         start_up()
 
-    for copy in (stress_in[1], stress_in[2], stress_in[5], velocity_in):
-        copy.wait()
-    when(x_low, lambda: arrived(halo_s.at[0], s_recv.at[0]))
-    when(x_high, lambda: arrived(halo_s.at[1], s_recv.at[1]))
-    join(halo_s, 0, NY)
-    def wait_stress_z(part, condition):
-        _, first, rows = z_parts[part]
-        to = pl.ds(8 + first, rows)
-        when(condition & z_low, lambda: arrived(sigma.at[:, 0:2, to, :], zs_recv.at[0, part]))
-        when(condition & z_high, lambda: arrived(sigma.at[:, 18:20, to, :], zs_recv.at[1, part]))
-
-    gap_copy = remote(gap_out, gap_in, gap_sem.at[0], gap_sem.at[1], down_y)
-    sends.append((after_gap, gap_copy))
-
-    def gap_package():
-        top = lax.broadcasted_iota(jnp.int32, (8, NX), 0) == 0
-
-        def layers_of(step, carry):
-            for k in (2 * step, 2 * step + 1):
-                scale = props[0, k, 0:8, :]
-                for c in range(6):
-                    gap_out[3 + c, k] = (scale * d_k(sigma, c, k, 0, 8))[0:2]
-                gap_out[9, k] = scale[0:2]
-                for i, (c_x, c_y) in enumerate(zip(X_PARTS, Y_PARTS)):
-                    here, after_1, after_2 = (sigma[c_y, k + 2, 8 + d : 16 + d, :] for d in range(3))
-                    before_1 = jnp.where(top, 0.0, pltpu.roll(here, 1, 0))
-                    grad_y = 8.0 * (after_1 - before_1) - after_2
-                    known = v_out[i, k, 0:8, :] + scale * (d_x(c_x, k, 0, 8, halo_s, i) + grad_y)
-                    gap_out[i, k] = known[0:2]
-            return carry
-
-        lax.fori_loop(0, NZ // 2, layers_of, 0)
-        gap_copy.start()
-
     def gap_velocity():
         arrived(gap_in, gap_sem.at[1])
 
@@ -454,36 +465,29 @@
             wide[part, 48:64, :] = jnp.zeros((16, NX), jnp.float32)
         metrics(NY, 8)
 
-    wait_stress_z(2, after_gap)
-    when(after_gap, gap_package)
     wait_stress_z(0, z >= 0)
     velocity_rows(8, 16, 2)
     send_rows(0, 8, 16)
     differentiate_x(range(3), vel, 8, 16, 4)
     when(before_gap, start_far)
+    when(before_gap, lambda: arrived(gap_terrain, gap_sem.at[3]))
+    for d in range(1, GZ):
+        send(before_gap, remote(gap_terrain, gap_terrain, pass_send.at[d - 1], pass_recv.at[own_slot], {"gz": (z + d) % GZ}))
+    for g in range(GZ):
+        send(before_gap & x_high & (z == GZ - 1), remote(gap_terrain, terrain.at[0, 40:48, :], pass_send.at[3 + g], pass_recv.at[0], {"gx": x + 1, "gz": g}))
+        send(before_gap & x_low & (z == 0), remote(gap_terrain, terrain.at[5, 40:48, :], pass_send.at[3 + g], pass_recv.at[5], {"gx": x - 1, "gz": g}))
+
+    def gap_terrain_arrived():
+        for d in range(1, GZ):
+            slot = 1 + (z + d) % GZ
+            arrived(terrain.at[slot, 40:48, :], pass_recv.at[slot])
+        when(x_low, lambda: arrived(terrain.at[0, 40:48, :], pass_recv.at[0]))
+        when(x_high, lambda: arrived(terrain.at[5, 40:48, :], pass_recv.at[5]))
 
     low_copy = remote(vel.at[:, 2:18, 8:10, :], vel.at[:, 2:18, 40:42, :], vy_send.at[1], vy_recv.at[1], down_y)
     high_copy = remote(vel.at[:, 2:18, 38:40, :], vel.at[:, 2:18, 6:8, :], vy_send.at[0], vy_recv.at[0], up_y)
     sends.append((y_low & ~after_gap, low_copy))
     sends.append((y_high, high_copy))
-    for part, low, first, outer in strips:
-        when(low & y_low, lambda: arrived(terrain.at[:, 0:8, :], edge_recv.at[0]))
-        when(~low & y_high, lambda: arrived(terrain.at[:, 40:48, :], edge_recv.at[1]))
-        heights(outer)
-        metrics(first, 8)
-        for i, c in enumerate(Y_SENT):
-            when(low & y_low, lambda: arrived(sigma.at[c, 2:18, 6:8, :], y_recv.at[0, i]))
-            when(~low & y_high, lambda: arrived(sigma.at[c, 2:18, 40:42, :], y_recv.at[1, i]))
-        wait_stress_z(part, (z >= 0) if part == 1 else ~after_gap)
-        velocity_rows(first, 8, 4)
-        when(low & y_low & ~after_gap, low_copy.start)
-        when(~low & y_high, high_copy.start)
-        send_rows(part, first, 8)
-    for _, _, first, _ in strips:
-        differentiate_x(range(3), vel, first, 8, 8)
-    when(before_gap, gap_metrics)
-
-    memory_in.wait()
 
     def stress_rows(first, rows, unroll, steps, stride=1):
         at = pl.ds(first, rows)
@@ -515,11 +519,8 @@
 
         lax.fori_loop(steps[0], steps[1], stress_layer, 0)
 
-    wait_x(0, 8, 16)
-    stress_rows(8, 16, 2, (1, NZ // 2 - 1))
-    wait_z(0, 8, 16)
-    stress_rows(8, 16, 2, (0, 2), NZ // 2 - 1)
-    for part, low, first, outer in strips:
+    def stress_beside(part):
+        _, low, first, _ = strips[part - 1]
         wait_x(part, first, 8)
         wait_z(part, first, 8)
         when(low & y_low, lambda: arrived(vel.at[:, 2:18, 6:8, :], vy_recv.at[0]))
@@ -527,6 +528,49 @@
         if part == 2:
             when(before_gap, gap_velocity)
         stress_rows(first, 8, 4, (0, NZ // 4))
+
+    inner_near = pl.multiple_of(16 - 8 * odd, 8)
+    inner_far = pl.multiple_of(8 + 8 * odd, 8)
+
+    def early_stress():
+        differentiate_x(range(3), vel, strips[0][2], 8, 8)
+        memory_in.wait()
+        wait_x(0, 8, 16)
+        wait_z(0, 8, 16)
+        stress_rows(inner_near, 8, 4, (0, NZ // 4))
+        stress_beside(1)
+
+    def late_stress():
+        differentiate_x(range(3), vel, strips[0][2], 8, 8)
+        memory_in.wait()
+        wait_x(0, 8, 16)
+        stress_rows(8, 16, 2, (1, NZ // 2 - 1))
+        wait_z(0, 8, 16)
+        stress_rows(8, 16, 2, (0, 2), NZ // 2 - 1)
+        stress_beside(1)
+
+    for part, low, first, outer in strips:
+        if part == 2:
+            when(at_gap, early_stress)
+        when(low & y_low, lambda: arrived(terrain.at[:, 0:8, :], edge_recv.at[0]))
+        when(~low & y_high & ~before_gap, lambda: arrived(terrain.at[:, 40:48, :], edge_recv.at[1]))
+        if part == 2:
+            when(before_gap, gap_terrain_arrived)
+        heights(outer)
+        metrics(first, 8)
+        for i, c in enumerate(Y_SENT):
+            when(low & y_low, lambda: arrived(sigma.at[c, 2:18, 6:8, :], y_recv.at[0, i]))
+            when(~low & y_high, lambda: arrived(sigma.at[c, 2:18, 40:42, :], y_recv.at[1, i]))
+        wait_stress_z(part, (z >= 0) if part == 1 else ~after_gap)
+        velocity_rows(first, 8, 4)
+        when(low & y_low & ~after_gap, low_copy.start)
+        when(~low & y_high, high_copy.start)
+        send_rows(part, first, 8)
+    differentiate_x(range(3), vel, strips[1][2], 8, 8)
+    when(before_gap, gap_metrics)
+    when(~at_gap, late_stress)
+    when(at_gap, lambda: stress_rows(inner_far, 8, 4, (0, NZ // 4)))
+    stress_beside(2)
     for condition, copy in sends:
         when(condition, copy.wait_send)
 
@@ -571,7 +615,7 @@
             dma((2, 3)), dma((2, 3)),
             vmem((10, NZ, 2, NX), f32),
             vmem((10, NZ, 2, NX), f32),
-            dma((2,)),
+            dma((4,)), dma((7,)), dma((6,)),
             pltpu.SemaphoreType.REGULAR,
         ],
         compiler_params=pltpu.CompilerParams(

time: 28.4 us -> 26.7 us (0.940)
  the two profiles are of different devices: /device:TPU:39 before, /device:TPU:192 now
where the time goes in v6:
time: 26.7 us; the launch traced here: 26.6 us
  Pallas kernels  26 us (97%)
  between operations  0.64 us (2%)
    pallas_call x1, Pallas kernels, local(): pl.pallas_call(kernel, out_shape=tuple((vmem(shape, f32) for shape in out...  23.9 us
    pallas_call x1, Pallas kernels, local(): pl.pallas_call(write_out, out_shape=tuple((jax.ShapeDtypeStruct(shape, f3...  2.04 us

profile of v6, /device:TPU:192, one launch (start us, length us, event | category | flops | bytes accessed | tf_op | source)
XLA Modules:
  0.0 26.6 jit_solution(18304009709009119233)
XLA Ops:
  0.6 23.9 %shard_map.139 = (f32[3,16,32,128]{3,2,1,0:T(8,128)S(1)}, f32[6,16,32,128]{3,2,1,0:T(8,128)S(1)}, f32[6,16,32,128]{3,2,1,0:T(8,128)S(1)}) custom-call(s32[32,32]{1,0:T(8,128)} %elevation.1, f32[16]{0:T(128)} %layer_base.1, f32[16]{0:T(128)} %stretch.1, s32[16,32,128]{2,1,0:T(8,128)} %material.1, f32[16]{0:T(128)} %buoyancy.1, f32[16]{0:T(128)} %lame.1, ...), custom_call_target="tpu_custom_call" | custom-call | tf_op jit(solution)/shard_map/pallas_call | solution.py:591
  24.6 2.0 %shard_map.140 = (f32[3,16,32,128]{3,2,1,0:T(8,128)}, f32[6,16,32,128]{3,2,1,0:T(8,128)}, f32[6,16,32,128]{3,2,1,0:T(8,128)}) custom-call(f32[3,16,32,128]{3,2,1,0:T(8,128)S(1)} %get-tuple-element.6.v_in, f32[6,16,32,128]{3,2,1,0:T(8,128)S(1)} %get-tuple-element.7.s_in, f32[6,16,32,128]{3,2,1,0:T(8,128)S(1)} %get-tuple-element.8.m_in), custom_call_target="tpu_custom_call" | custom-call | tf_op jit(solution)/shard_map/pallas_call | solution.py:625

commit v7 on v6

--- a/solution.py
+++ b/solution.py
@@ -127,10 +127,10 @@
         when(z_high if condition is None else condition & z_high, z_copies[part][0].start)
         when(z_low if condition is None else condition & z_low, z_copies[part][1].start)
 
-    start_z(2, after_gap)
+    start_z(2, at_gap)
     start_z(0, None)
     start_z(1, None)
-    start_z(2, ~after_gap)
+    start_z(2, ~at_gap)
 
     zero = jnp.zeros((8, NX), jnp.float32)
 
@@ -285,31 +285,40 @@
         when(condition & z_low, lambda: arrived(sigma.at[:, 0:2, to, :], zs_recv.at[0, part]))
         when(condition & z_high, lambda: arrived(sigma.at[:, 18:20, to, :], zs_recv.at[1, part]))
 
-    gap_copy = remote(gap_out, gap_in, gap_sem.at[0], gap_sem.at[1], down_y)
-    sends.append((after_gap, gap_copy))
-
-    def gap_package():
-        top = lax.broadcasted_iota(jnp.int32, (8, NX), 0) == 0
+    gap_down = remote(gap_out, gap_in, gap_sem.at[0], gap_sem.at[1], down_y)
+    gap_up = remote(gap_out, gap_in, gap_sem.at[0], gap_sem.at[1], up_y)
+    sends.append((after_gap, gap_down))
+    sends.append((before_gap, gap_up))
+
+    def gap_package(first, kept):
+        row = lax.broadcasted_iota(jnp.int32, (8, NX), 0)
 
         def layers_of(step, carry):
             for k in (2 * step, 2 * step + 1):
-                scale = props[0, k, 0:8, :]
+                scale = props[0, k, first : first + 8, :]
                 for c in range(6):
-                    gap_out[3 + c, k] = (scale * d_k(sigma, c, k, 0, 8))[0:2]
-                gap_out[9, k] = scale[0:2]
+                    gap_out[3 + c, k] = (scale * d_k(sigma, c, k, first, 8))[kept]
+                gap_out[9, k] = scale[kept]
                 for i, (c_x, c_y) in enumerate(zip(X_PARTS, Y_PARTS)):
-                    here, after_1, after_2 = (sigma[c_y, k + 2, 8 + d : 16 + d, :] for d in range(3))
-                    before_1 = jnp.where(top, 0.0, pltpu.roll(here, 1, 0))
-                    grad_y = 8.0 * (after_1 - before_1) - after_2
-                    known = v_out[i, k, 0:8, :] + scale * (d_x(c_x, k, 0, 8, halo_s, i) + grad_y)
-                    gap_out[i, k] = known[0:2]
+                    if first == 0:
+                        here, beside_1, beside_2 = (sigma[c_y, k + 2, 8 + d : 16 + d, :] for d in range(3))
+                        grad_y = 8.0 * (beside_1 - jnp.where(row == 0, 0.0, pltpu.roll(here, 1, 0))) - beside_2
+                    else:
+                        here, beside_1, beside_2 = (sigma[c_y, k + 2, 32 - d : 40 - d, :] for d in range(3))
+                        grad_y = 8.0 * (jnp.where(row == 7, 0.0, pltpu.roll(here, 7, 0)) - beside_1) + beside_2
+                    known = v_out[i, k, first : first + 8, :] + scale * (d_x(c_x, k, first, 8, halo_s, i) + grad_y)
+                    gap_out[i, k] = known[kept]
             return carry
 
         lax.fori_loop(0, NZ // 2, layers_of, 0)
-        gap_copy.start()
-
-    wait_stress_z(2, after_gap)
-    when(after_gap, gap_package)
+
+    def package_down():
+        gap_package(0, slice(0, 2))
+        gap_down.start()
+
+    wait_stress_z(2, at_gap)
+    when(after_gap, package_down)
+    when(before_gap, lambda: gap_package(24, slice(6, 8)))
 
     elevation_in.wait()
     for d in range(1, GZ):
@@ -322,8 +331,8 @@
     send(y_low & ~after_gap, remote(terrain.at[:, 8:16, :], terrain.at[:, 40:48, :], edge_send.at[1], edge_recv.at[1], down_y))
 
     def heights(row):
-        rows = pl.ds(row, 8)
-        held = [terrain[m, rows, :].astype(jnp.float32) / 200.0 for m in range(6)]
+        held = [terrain[m, pl.ds(row, 8), :].astype(jnp.float32) / 200.0 for m in range(6)]
+        rows = pl.ds(row + 8, 8)
         blank = jnp.zeros((8, 96), jnp.float32)
         wide[0, rows, :] = jnp.concatenate([blank, held[0]], axis=1)
         wide[1, rows, :] = jnp.concatenate(held[1:5], axis=1)
@@ -336,7 +345,7 @@
         for part in range(3):
             total = jnp.zeros((rows + 8, NX), jnp.float32)
             for d, factor in enumerate(binomial):
-                total = total + factor * wide[part, pl.ds(first + 2 + d, rows + 8), :]
+                total = total + factor * wide[part, pl.ds(first + 10 + d, rows + 8), :]
             along_y.append(total / 16.0)
         row = jnp.concatenate(along_y, axis=1)
         total = jnp.zeros_like(row)
@@ -366,7 +375,7 @@
                 weighted = follow * thickness
                 inverse = 1.0 / thickness
                 factor = (total + 0.5 * weighted - 1.0) * inverse
-                at = pl.ds(first, rows)
+                at = pl.ds(8 + first, rows)
                 metric[0, k, at, :] = slope_x * factor
                 metric[1, k, at, :] = slope_y * factor
                 metric[2, k, at, :] = inverse
@@ -385,7 +394,7 @@
             pack_rows(held, [k - unroll for k in ks], last)
             made = []
             for k in ks:
-                m_x, m_y, m_z = (metric[i, k, at, :] for i in range(3))
+                m_x, m_y, m_z = (metric[i, k, pl.ds(8 + first, rows), :] for i in range(3))
                 grad_k = [d_k(sigma, c, k, first, rows) for c in range(6)]
                 grad_x = [d_x(c, k, first, rows, halo_s, i) for i, c in enumerate(X_PARTS)]
                 grad_y = [d_y(sigma, c, k, first, rows) for c in Y_PARTS]
@@ -444,26 +453,31 @@
         pl.semaphore_wait(far_sem, 1)
         edge_up.start()
         start_up()
-
-    def gap_velocity():
+        gap_up.start()
+
+    def gap_velocity(row, own):
         arrived(gap_in, gap_sem.at[1])
 
         def layers_of(step, carry):
             for k in (2 * step, 2 * step + 1):
-                m_x, m_y, m_z = (metric[i, k, NY : NY + 2, :] for i in range(3))
+                m_x, m_y, m_z = (metric[i, k, 8 + row : 10 + row, :] for i in range(3))
                 for i, (a, b, d) in enumerate(((0, 3, 4), (3, 1, 5), (4, 5, 2))):
-                    edge = sigma[Y_PARTS[i], k + 2, 38:40, :]
-                    beyond = jnp.concatenate([edge[0:1] - 8.0 * edge[1:2], edge[1:2]], axis=0)
+                    edge = sigma[Y_PARTS[i], k + 2, 8 + own : 10 + own, :]
+                    if own:
+                        beyond = jnp.concatenate([edge[0:1] - 8.0 * edge[1:2], edge[1:2]], axis=0)
+                    else:
+                        beyond = jnp.concatenate([-edge[0:1], 8.0 * edge[0:1] - edge[1:2]], axis=0)
                     known = gap_in[i, k] + gap_in[9, k] * beyond
-                    vel[i, 2 + k, 40:42, :] = known - m_x * gap_in[3 + a, k] - m_y * gap_in[3 + b, k] + m_z * gap_in[3 + d, k]
+                    new = known - m_x * gap_in[3 + a, k] - m_y * gap_in[3 + b, k] + m_z * gap_in[3 + d, k]
+                    vel[i, 2 + k, 8 + row : 10 + row, :] = new
             return carry
 
         lax.fori_loop(0, NZ // 2, layers_of, 0)
 
-    def gap_metrics():
+    def gap_metrics(first, blank):
         for part in range(3):
-            wide[part, 48:64, :] = jnp.zeros((16, NX), jnp.float32)
-        metrics(NY, 8)
+            wide[part, blank, :] = jnp.zeros((8, NX), jnp.float32)
+        metrics(first, 8)
 
     wait_stress_z(0, z >= 0)
     velocity_rows(8, 16, 2)
@@ -487,7 +501,7 @@
     low_copy = remote(vel.at[:, 2:18, 8:10, :], vel.at[:, 2:18, 40:42, :], vy_send.at[1], vy_recv.at[1], down_y)
     high_copy = remote(vel.at[:, 2:18, 38:40, :], vel.at[:, 2:18, 6:8, :], vy_send.at[0], vy_recv.at[0], up_y)
     sends.append((y_low & ~after_gap, low_copy))
-    sends.append((y_high, high_copy))
+    sends.append((y_high & ~before_gap, high_copy))
 
     def stress_rows(first, rows, unroll, steps, stride=1):
         at = pl.ds(first, rows)
@@ -495,7 +509,7 @@
         def stress_layer(step, carry):
             for k in [unroll * stride * step + i for i in range(unroll)]:
                 grad_x = [d_x(c, k, first, rows, halo_v, c) for c in range(3)]
-                m_x, m_y, m_z = (metric[i, k, at, :] for i in range(3))
+                m_x, m_y, m_z = (metric[i, k, pl.ds(8 + first, rows), :] for i in range(3))
                 along_k = [d_k(vel, c, k, first, rows) for c in range(3)]
                 along_x = [grad_x[c] - m_x * along_k[c] for c in range(3)]
                 along_y = [d_y(vel, c, k, first, rows) - m_y * along_k[c] for c in range(3)]
@@ -523,10 +537,11 @@
         _, low, first, _ = strips[part - 1]
         wait_x(part, first, 8)
         wait_z(part, first, 8)
-        when(low & y_low, lambda: arrived(vel.at[:, 2:18, 6:8, :], vy_recv.at[0]))
+        when(low & y_low & ~after_gap, lambda: arrived(vel.at[:, 2:18, 6:8, :], vy_recv.at[0]))
         when(~low & y_high & ~before_gap, lambda: arrived(vel.at[:, 2:18, 40:42, :], vy_recv.at[1]))
         if part == 2:
-            when(before_gap, gap_velocity)
+            when(before_gap, lambda: gap_velocity(NY, NY - 2))
+            when(after_gap, lambda: gap_velocity(-2, 0))
         stress_rows(first, 8, 4, (0, NZ // 4))
 
     inner_near = pl.multiple_of(16 - 8 * odd, 8)
@@ -561,13 +576,14 @@
         for i, c in enumerate(Y_SENT):
             when(low & y_low, lambda: arrived(sigma.at[c, 2:18, 6:8, :], y_recv.at[0, i]))
             when(~low & y_high, lambda: arrived(sigma.at[c, 2:18, 40:42, :], y_recv.at[1, i]))
-        wait_stress_z(part, (z >= 0) if part == 1 else ~after_gap)
+        wait_stress_z(part, (z >= 0) if part == 1 else ~at_gap)
         velocity_rows(first, 8, 4)
         when(low & y_low & ~after_gap, low_copy.start)
-        when(~low & y_high, high_copy.start)
+        when(~low & y_high & ~before_gap, high_copy.start)
         send_rows(part, first, 8)
     differentiate_x(range(3), vel, strips[1][2], 8, 8)
-    when(before_gap, gap_metrics)
+    when(before_gap, lambda: gap_metrics(NY, slice(56, 64)))
+    when(after_gap, lambda: gap_metrics(-8, slice(0, 8)))
     when(~at_gap, late_stress)
     when(at_gap, lambda: stress_rows(inner_far, 8, 4, (0, NZ // 4)))
     stress_beside(2)
@@ -605,7 +621,7 @@
             vmem((5, NZ, NY, NX), f32),
             vmem((NX, NX), jnp.bfloat16),
             vmem((3, NZ, NY, NX), f32),
-            vmem((3, NZ, NY + 8, NX), f32),
+            vmem((3, NZ, NY + 16, NX), f32),
             vmem((2, 2, NY, NX), f32),
             vmem((2, 2, NY, NX), f32),
             vmem((2, 2, NY, NX), f32),

time: 26.7 us -> 29.2 us (1.094)
  the two profiles are of different devices: /device:TPU:192 before, /device:TPU:7 now
where the time goes in v7:
time: 29.2 us; the launch traced here: 29.1 us
  Pallas kernels  28.5 us (98%)
  between operations  0.64 us (2%)
    pallas_call x1, Pallas kernels, local(): pl.pallas_call(kernel, out_shape=tuple((vmem(shape, f32) for shape in out...  26.4 us
    pallas_call x1, Pallas kernels, local(): pl.pallas_call(write_out, out_shape=tuple((jax.ShapeDtypeStruct(shape, f3...  2.04 us

profile of v7, /device:TPU:7, one launch (start us, length us, event | category | flops | bytes accessed | tf_op | source)
XLA Modules:
  0.0 29.1 jit_solution(6252746795166289830)
XLA Ops:
  0.6 26.4 %shard_map.139 = (f32[3,16,32,128]{3,2,1,0:T(8,128)S(1)}, f32[6,16,32,128]{3,2,1,0:T(8,128)S(1)}, f32[6,16,32,128]{3,2,1,0:T(8,128)S(1)}) custom-call(s32[32,32]{1,0:T(8,128)} %elevation.1, f32[16]{0:T(128)} %layer_base.1, f32[16]{0:T(128)} %stretch.1, s32[16,32,128]{2,1,0:T(8,128)} %material.1, f32[16]{0:T(128)} %buoyancy.1, f32[16]{0:T(128)} %lame.1, ...), custom_call_target="tpu_custom_call" | custom-call | tf_op jit(solution)/shard_map/pallas_call | solution.py:607
  27.1 2.0 %shard_map.140 = (f32[3,16,32,128]{3,2,1,0:T(8,128)}, f32[6,16,32,128]{3,2,1,0:T(8,128)}, f32[6,16,32,128]{3,2,1,0:T(8,128)}) custom-call(f32[3,16,32,128]{3,2,1,0:T(8,128)S(1)} %get-tuple-element.6.v_in, f32[6,16,32,128]{3,2,1,0:T(8,128)S(1)} %get-tuple-element.7.s_in, f32[6,16,32,128]{3,2,1,0:T(8,128)S(1)} %get-tuple-element.8.m_in), custom_call_target="tpu_custom_call" | custom-call | tf_op jit(solution)/shard_map/pallas_call | solution.py:641

commit v8 on v6

--- a/solution.py
+++ b/solution.py
@@ -465,11 +465,11 @@
             wide[part, 48:64, :] = jnp.zeros((16, NX), jnp.float32)
         metrics(NY, 8)
 
+    when(before_gap, start_far)
     wait_stress_z(0, z >= 0)
     velocity_rows(8, 16, 2)
     send_rows(0, 8, 16)
     differentiate_x(range(3), vel, 8, 16, 4)
-    when(before_gap, start_far)
     when(before_gap, lambda: arrived(gap_terrain, gap_sem.at[3]))
     for d in range(1, GZ):
         send(before_gap, remote(gap_terrain, gap_terrain, pass_send.at[d - 1], pass_recv.at[own_slot], {"gz": (z + d) % GZ}))
@@ -538,7 +538,6 @@
         wait_x(0, 8, 16)
         wait_z(0, 8, 16)
         stress_rows(inner_near, 8, 4, (0, NZ // 4))
-        stress_beside(1)
 
     def late_stress():
         differentiate_x(range(3), vel, strips[0][2], 8, 8)
@@ -547,7 +546,6 @@
         stress_rows(8, 16, 2, (1, NZ // 2 - 1))
         wait_z(0, 8, 16)
         stress_rows(8, 16, 2, (0, 2), NZ // 2 - 1)
-        stress_beside(1)
 
     for part, low, first, outer in strips:
         if part == 2:
@@ -570,6 +568,7 @@
     when(before_gap, gap_metrics)
     when(~at_gap, late_stress)
     when(at_gap, lambda: stress_rows(inner_far, 8, 4, (0, NZ // 4)))
+    stress_beside(1)
     stress_beside(2)
     for condition, copy in sends:
         when(condition, copy.wait_send)

time: 26.7 us -> 25.4 us (0.951)
  Pallas kernels: 26 us -> 24.7 us
    pallas_call x1, Pallas kernels: 23.9 us -> 22.7 us  [local(): pl.pallas_call(kernel, out_shape=tuple((vmem(shape, f32) for shape in out...]
where the time goes in v8:
time: 25.4 us
  Pallas kernels  24.7 us (97%)
  between operations  0.64 us (3%)
    pallas_call x1, Pallas kernels, local(): pl.pallas_call(kernel, out_shape=tuple((vmem(shape, f32) for shape in out...  22.7 us
    pallas_call x1, Pallas kernels, local(): pl.pallas_call(write_out, out_shape=tuple((jax.ShapeDtypeStruct(shape, f3...  2.04 us

profile of v8, /device:TPU:192, one launch (start us, length us, event | category | flops | bytes accessed | tf_op | source)
XLA Modules:
  0.0 25.4 jit_solution(4871769461279151572)
XLA Ops:
  0.6 22.7 %shard_map.139 = (f32[3,16,32,128]{3,2,1,0:T(8,128)S(1)}, f32[6,16,32,128]{3,2,1,0:T(8,128)S(1)}, f32[6,16,32,128]{3,2,1,0:T(8,128)S(1)}) custom-call(s32[32,32]{1,0:T(8,128)} %elevation.1, f32[16]{0:T(128)} %layer_base.1, f32[16]{0:T(128)} %stretch.1, s32[16,32,128]{2,1,0:T(8,128)} %material.1, f32[16]{0:T(128)} %buoyancy.1, f32[16]{0:T(128)} %lame.1, ...), custom_call_target="tpu_custom_call" | custom-call | tf_op jit(solution)/shard_map/pallas_call | solution.py:590
  23.3 2.0 %shard_map.140 = (f32[3,16,32,128]{3,2,1,0:T(8,128)}, f32[6,16,32,128]{3,2,1,0:T(8,128)}, f32[6,16,32,128]{3,2,1,0:T(8,128)}) custom-call(f32[3,16,32,128]{3,2,1,0:T(8,128)S(1)} %get-tuple-element.6.v_in, f32[6,16,32,128]{3,2,1,0:T(8,128)S(1)} %get-tuple-element.7.s_in, f32[6,16,32,128]{3,2,1,0:T(8,128)S(1)} %get-tuple-element.8.m_in), custom_call_target="tpu_custom_call" | custom-call | tf_op jit(solution)/shard_map/pallas_call | solution.py:624

commit v9 on v8

--- a/solution.py
+++ b/solution.py
@@ -27,10 +27,49 @@
     return 8.0 * (after_1 - before_1) - (after_2 - before_2)
 
 
+def d_k(field, c, k, first, rows):
+    return centred_12(*[field[c, k + 2 + d, pl.ds(8 + first, rows), :] for d in (-2, -1, 1, 2)])
+
+
+def d_y(field, c, k, first, rows):
+    return centred_12(*[field[c, k + 2, pl.ds(8 + first + d, rows), :] for d in (-2, -1, 1, 2)])
+
+
+def d_x_of(along, c, k, first, rows, halo, i):
+    side = lax.broadcasted_iota(jnp.int32, (rows, NX), 1)
+    at = 4 * (k + (NZ if i == 1 else 0))
+    fix = pltpu.roll(halo[0, i // 2, pl.ds(first, rows), :], 126 - at, 1)
+    return along[i, k, pl.ds(first, rows), :] + jnp.where((side < 2) | (side >= 126), fix, 0.0)
+
+
+def stress_layer_of(memory, sigma, vel, along, halo_v, metric, props, k, first, rows):
+    at = pl.ds(first, rows)
+    grad_x = [d_x_of(along, c, k, first, rows, halo_v, c) for c in range(3)]
+    m_x, m_y, m_z = (metric[i, k, at, :] for i in range(3))
+    along_k = [d_k(vel, c, k, first, rows) for c in range(3)]
+    along_x = [grad_x[c] - m_x * along_k[c] for c in range(3)]
+    along_y = [d_y(vel, c, k, first, rows) - m_y * along_k[c] for c in range(3)]
+    along_z = [m_z * along_k[c] for c in range(3)]
+    lam, mu, kept, gain = (props[i, k, at, :] for i in range(1, 5))
+    volume = lam * (along_x[0] + along_y[1] + along_z[2])
+    twice = mu + mu
+    rates = (
+        volume + twice * along_x[0],
+        volume + twice * along_y[1],
+        volume + twice * along_z[2],
+        mu * (along_y[0] + along_x[1]),
+        mu * (along_z[0] + along_x[2]),
+        mu * (along_z[1] + along_y[2]),
+    )
+    for c, rate in enumerate(rates):
+        new = kept * memory[c, k, at, :] + gain * rate
+        yield c, new, sigma[c, 2 + k, pl.ds(8 + first, rows), :] + STEP * (rate - new)
+
+
 def kernel(
     elevation, layer_base, stretch, material, buoyancy, lame, shear, relax, weight, velocity, stress, memory,
-    v_out, s_out, m_out,
-    sigma, vel, terrain, wide, surf, layers, mat, tables, props, stencil, along, metric, packs, halo_s, halo_v,
+    v_out, s_out, m_out, sigma, vel, along, halo_v, metric, props,
+    terrain, wide, surf, layers, mat, tables, stencil, packs, halo_s,
     small, local_sem, s_send, s_recv, y_send, y_recv, layer_send, layer_recv, t_send, t_recv, edge_send, edge_recv,
     z_send, z_recv, x_send, x_recv, vy_send, vy_recv, zs_send, zs_recv, gap_out, gap_in, gap_sem, pass_send, pass_recv, far_sem,
 ):
@@ -253,17 +292,7 @@
     when(x == 0, lambda: zero_x(0, 0))
     when(x == GX - 1, lambda: zero_x(1, 5))
 
-    def d_k(field, c, k, first, rows):
-        return centred_12(*[field[c, k + 2 + d, pl.ds(8 + first, rows), :] for d in (-2, -1, 1, 2)])
-
-    def d_y(field, c, k, first, rows):
-        return centred_12(*[field[c, k + 2, pl.ds(8 + first + d, rows), :] for d in (-2, -1, 1, 2)])
-
-    def d_x(c, k, first, rows, halo, i):
-        side = lax.broadcasted_iota(jnp.int32, (rows, NX), 1)
-        at = 4 * (k + (NZ if i == 1 else 0))
-        fix = pltpu.roll(halo[0, i // 2, pl.ds(first, rows), :], 126 - at, 1)
-        return along[i, k, pl.ds(first, rows), :] + jnp.where((side < 2) | (side >= 126), fix, 0.0)
+    d_x = functools.partial(d_x_of, along)
 
     def join(halo, first, rows):
         spot = lax.broadcasted_iota(jnp.int32, (rows, NX), 1) % 4
@@ -494,27 +523,9 @@
 
         def stress_layer(step, carry):
             for k in [unroll * stride * step + i for i in range(unroll)]:
-                grad_x = [d_x(c, k, first, rows, halo_v, c) for c in range(3)]
-                m_x, m_y, m_z = (metric[i, k, at, :] for i in range(3))
-                along_k = [d_k(vel, c, k, first, rows) for c in range(3)]
-                along_x = [grad_x[c] - m_x * along_k[c] for c in range(3)]
-                along_y = [d_y(vel, c, k, first, rows) - m_y * along_k[c] for c in range(3)]
-                along_z = [m_z * along_k[c] for c in range(3)]
-                lam, mu, kept, gain = (props[i, k, at, :] for i in range(1, 5))
-                volume = lam * (along_x[0] + along_y[1] + along_z[2])
-                twice = mu + mu
-                rates = (
-                    volume + twice * along_x[0],
-                    volume + twice * along_y[1],
-                    volume + twice * along_z[2],
-                    mu * (along_y[0] + along_x[1]),
-                    mu * (along_z[0] + along_x[2]),
-                    mu * (along_z[1] + along_y[2]),
-                )
-                for c, rate in enumerate(rates):
-                    new = kept * m_out[c, k, at, :] + gain * rate
+                for c, new, total in stress_layer_of(m_out, sigma, vel, along, halo_v, metric, props, k, first, rows):
                     m_out[c, k, at, :] = new
-                    s_out[c, k, at, :] = sigma[c, 2 + k, pl.ds(8 + first, rows), :] + STEP * (rate - new)
+                    s_out[c, k, at, :] = total
             return carry
 
         lax.fori_loop(steps[0], steps[1], stress_layer, 0)
@@ -527,7 +538,8 @@
         when(~low & y_high & ~before_gap, lambda: arrived(vel.at[:, 2:18, 40:42, :], vy_recv.at[1]))
         if part == 2:
             when(before_gap, gap_velocity)
-        stress_rows(first, 8, 4, (0, NZ // 4))
+        if part == 1:
+            stress_rows(first, 8, 4, (0, NZ // 4))
 
     inner_near = pl.multiple_of(16 - 8 * odd, 8)
     inner_far = pl.multiple_of(8 + 8 * odd, 8)
@@ -574,12 +586,32 @@
         when(condition, copy.wait_send)
 
 
-def write_out(v_in, s_in, m_in, v_ref, s_ref, m_ref, sems):
-    pairs = [(v_in, v_ref, c) for c in range(3)] + [(a, b, c) for a, b in ((s_in, s_ref), (m_in, m_ref)) for c in range(6)]
-    copies = [pltpu.make_async_copy(a.at[c], b.at[c], sems.at[i]) for i, (a, b, c) in enumerate(pairs)]
+def write_out(v_in, s_in, m_in, sigma, vel, along, halo_v, metric, props, v_ref, s_ref, m_ref, last, sems):
+    odd = lax.axis_index("gy") % 2
+    first = pl.multiple_of(24 * odd, 8)
+    strip, rest = pl.ds(first, 8), pl.ds(pl.multiple_of(8 - 8 * odd, 8), 24)
+    copies = [pltpu.make_async_copy(v_in.at[c], v_ref.at[c], sems.at[c]) for c in range(3)]
+    for c in range(6):
+        copies.append(pltpu.make_async_copy(s_in.at[c, :, rest, :], s_ref.at[c, :, rest, :], sems.at[3 + c]))
+        copies.append(pltpu.make_async_copy(m_in.at[c, :, rest, :], m_ref.at[c, :, rest, :], sems.at[9 + c]))
     for copy in copies:
         copy.start()
-    for copy in copies:
+
+    def layers_of(step, carry):
+        for k in [4 * step + i for i in range(4)]:
+            for c, new, total in stress_layer_of(m_in, sigma, vel, along, halo_v, metric, props, k, first, 8):
+                last[c, k] = total
+                last[6 + c, k] = new
+        return carry
+
+    lax.fori_loop(0, NZ // 4, layers_of, 0)
+    late = []
+    for c in range(6):
+        late.append(pltpu.make_async_copy(last.at[c], s_ref.at[c, :, strip, :], sems.at[15 + c]))
+        late.append(pltpu.make_async_copy(last.at[6 + c], m_ref.at[c, :, strip, :], sems.at[21 + c]))
+    for copy in late:
+        copy.start()
+    for copy in copies + late:
         copy.wait()
 
 
@@ -587,25 +619,20 @@
     held = [pltpu.with_memory_space_constraint(array, pltpu.HBM) for array in arrays]
     f32, vmem, dma = jnp.float32, pltpu.VMEM, pltpu.SemaphoreType.DMA
     outputs = [(n, NZ, NY, NX) for n in (3, 6, 6)]
+    kept = [(6, 20, 48, NX), (3, 20, 48, NX), (3, NZ, NY, NX), (2, 2, NY, NX), (3, NZ, NY + 8, NX), (5, NZ, NY, NX)]
     results = pl.pallas_call(
         kernel,
-        out_shape=tuple(vmem(shape, f32) for shape in outputs),
+        out_shape=tuple(vmem(shape, f32) for shape in outputs + kept),
         in_specs=[pl.BlockSpec(memory_space=pltpu.HBM)] * len(held),
-        out_specs=tuple(pl.BlockSpec(memory_space=vmem) for _ in outputs),
+        out_specs=tuple(pl.BlockSpec(memory_space=vmem) for _ in outputs + kept),
         scratch_shapes=[
-            vmem((6, 20, 48, NX), f32),
-            vmem((3, 20, 48, NX), f32),
             vmem((6, 48, 32), jnp.int32),
             vmem((3, 64, NX), f32),
             vmem((3, 24, NX), f32),
             vmem((2, GZ * NZ, NX), f32),
             vmem((NZ, NY, NX), jnp.int32),
             vmem((5, 8, NX), f32),
-            vmem((5, NZ, NY, NX), f32),
             vmem((NX, NX), jnp.bfloat16),
-            vmem((3, NZ, NY, NX), f32),
-            vmem((3, NZ, NY + 8, NX), f32),
-            vmem((2, 2, NY, NX), f32),
             vmem((2, 2, NY, NX), f32),
             vmem((2, 2, NY, NX), f32),
             pltpu.SMEM((7, 16), f32),
@@ -624,9 +651,9 @@
     return pl.pallas_call(
         write_out,
         out_shape=tuple(jax.ShapeDtypeStruct(shape, f32) for shape in outputs),
-        in_specs=[pl.BlockSpec(memory_space=vmem)] * 3,
+        in_specs=[pl.BlockSpec(memory_space=vmem)] * 9,
         out_specs=tuple(pl.BlockSpec(memory_space=pltpu.HBM) for _ in outputs),
-        scratch_shapes=[dma((15,))],
+        scratch_shapes=[vmem((12, NZ, 8, NX), f32), dma((27,))],
         compiler_params=pltpu.CompilerParams(vmem_limit_bytes=8 << 20),
     )(*results)
 

time: 25.4 us -> 25.1 us (0.988)
  Pallas kernels: 24.7 us -> 24.4 us
    pallas_call x1, Pallas kernels: 22.7 us -> 22.2 us  [local(): pl.pallas_call(kernel, out_shape=tuple((vmem(shape, f32) for shape in out...]
where the time goes in v9:
time: 25.1 us; the launch traced here: 25 us
  Pallas kernels  24.4 us (97%)
  between operations  0.64 us (3%)
    pallas_call x1, Pallas kernels, local(): pl.pallas_call(kernel, out_shape=tuple((vmem(shape, f32) for shape in out...  22.2 us
    pallas_call x1, Pallas kernels, local(): pl.pallas_call(write_out, out_shape=tuple((jax.ShapeDtypeStruct(shape, f3...  2.14 us

profile of v9, /device:TPU:192, one launch (start us, length us, event | category | flops | bytes accessed | tf_op | source)
XLA Modules:
  0.0 25.0 jit_solution(4382089864344929333)
XLA Ops:
  0.6 22.2 %shard_map.139 = (f32[3,16,32,128]{3,2,1,0:T(8,128)S(1)}, f32[6,16,32,128]{3,2,1,0:T(8,128)S(1)}, f32[6,16,32,128]{3,2,1,0:T(8,128)S(1)}, f32[6,20,48,128]{3,2,1...) custom-call(s32[32,32]{1,0:T(8,128)} %elevation.1, ...), custom_call_target="tpu_custom_call" | custom-call | tf_op jit(solution)/shard_map/pallas_call | solution.py:623
  22.9 2.1 %shard_map.140 = (f32[3,16,32,128]{3,2,1,0:T(8,128)}, f32[6,16,32,128]{3,2,1,0:T(8,128)}, f32[6,16,32,128]{3,2,1,0:T(8,128)}) custom-call(f32[3,16,32,128]{3,2,1,0:T(8,128)S(1)} %get-tuple-element.12.v_in, f32[6,16,32,128]{3,2,1,0:T(8,128)S(1)} %get-tuple-element.13.s_in, f32[6,16,32,128]{3,2,1,0:T(8,128)S(1)} %get-tuple-element.14.m_in, ...), custom_call_target="tpu_custom_call" | custom-call | tf_op jit(solution)/shard_map/pallas_call | solution.py:651

commit v10 on v9

--- a/solution.py
+++ b/solution.py
@@ -81,6 +81,16 @@
     at_gap = before_gap | after_gap
     lane = lax.broadcasted_iota(jnp.int32, (8, NX), 1)
 
+    barrier = pltpu.get_barrier_semaphore()
+    beside = [(None, {"gz": (z + d) % GZ}) for d in range(1, GZ)]
+    for g in range(GZ):
+        beside.append((x_high & ((z == g) | (z == GZ - 1) | (g == 0)), {"gx": x + 1, "gz": g}))
+        beside.append((x_low & ((z == g) | (z == 0) | (g == GZ - 1)), {"gx": x - 1, "gz": g}))
+    up_y, down_y = {"gy": y + 1}, {"gy": y - 1}
+    for condition, target in [(y_high, up_y), (y_low & ~after_gap, down_y)] + beside:
+        when(condition, lambda target=target: pl.semaphore_signal(barrier, inc=1, device_id=target, device_id_type=MESH))
+    expected = [y_low, y_high & ~before_gap] + [condition for condition, _ in beside]
+
     own_slot = 1 + z
     tables_in = (buoyancy, lame, shear, relax, weight, layer_base, stretch)
     scalars = [pltpu.make_async_copy(ref, small.at[i], local_sem.at[i]) for i, ref in enumerate(tables_in)]
@@ -101,16 +111,6 @@
     memory_in = pltpu.make_async_copy(memory, m_out, local_sem.at[16])
     for copy in (elevation_in, velocity_in, memory_in):
         copy.start()
-
-    barrier = pltpu.get_barrier_semaphore()
-    beside = [(None, {"gz": (z + d) % GZ}) for d in range(1, GZ)]
-    for g in range(GZ):
-        beside.append((x_high & ((z == g) | (z == GZ - 1) | (g == 0)), {"gx": x + 1, "gz": g}))
-        beside.append((x_low & ((z == g) | (z == 0) | (g == GZ - 1)), {"gx": x - 1, "gz": g}))
-    up_y, down_y = {"gy": y + 1}, {"gy": y - 1}
-    for condition, target in [(y_high, up_y), (y_low & ~after_gap, down_y)] + beside:
-        when(condition, lambda target=target: pl.semaphore_signal(barrier, inc=1, device_id=target, device_id_type=MESH))
-    expected = [y_low, y_high & ~before_gap] + [condition for condition, _ in beside]
 
     pl.semaphore_wait(barrier, sum(1 if c is None else c.astype(jnp.int32) for c in expected))
     when(after_gap, lambda: pl.semaphore_signal(far_sem, inc=1, device_id=down_y, device_id_type=MESH))
@@ -561,7 +561,7 @@
 
     for part, low, first, outer in strips:
         if part == 2:
-            when(at_gap, early_stress)
+            when(before_gap, early_stress)
         when(low & y_low, lambda: arrived(terrain.at[:, 0:8, :], edge_recv.at[0]))
         when(~low & y_high & ~before_gap, lambda: arrived(terrain.at[:, 40:48, :], edge_recv.at[1]))
         if part == 2:
@@ -578,6 +578,7 @@
         send_rows(part, first, 8)
     differentiate_x(range(3), vel, strips[1][2], 8, 8)
     when(before_gap, gap_metrics)
+    when(after_gap, early_stress)
     when(~at_gap, late_stress)
     when(at_gap, lambda: stress_rows(inner_far, 8, 4, (0, NZ // 4)))
     stress_beside(1)

time: 25.1 us -> 25.1 us (level)
  no operation moved by 1% of the time
where the time goes in v10:
time: 25.1 us; the launch traced here: 25 us
  Pallas kernels  24.4 us (97%)
  between operations  0.64 us (3%)
    pallas_call x1, Pallas kernels, local(): pl.pallas_call(kernel, out_shape=tuple((vmem(shape, f32) for shape in out...  22.2 us
    pallas_call x1, Pallas kernels, local(): pl.pallas_call(write_out, out_shape=tuple((jax.ShapeDtypeStruct(shape, f3...  2.14 us

profile of v10, /device:TPU:192, one launch (start us, length us, event | category | flops | bytes accessed | tf_op | source)
XLA Modules:
  0.0 25.0 jit_solution(5355931465785721493)
XLA Ops:
  0.6 22.2 %shard_map.139 = (f32[3,16,32,128]{3,2,1,0:T(8,128)S(1)}, f32[6,16,32,128]{3,2,1,0:T(8,128)S(1)}, f32[6,16,32,128]{3,2,1,0:T(8,128)S(1)}, f32[6,20,48,128]{3,2,1...) custom-call(s32[32,32]{1,0:T(8,128)} %elevation.1, ...), custom_call_target="tpu_custom_call" | custom-call | tf_op jit(solution)/shard_map/pallas_call | solution.py:624
  22.9 2.1 %shard_map.140 = (f32[3,16,32,128]{3,2,1,0:T(8,128)}, f32[6,16,32,128]{3,2,1,0:T(8,128)}, f32[6,16,32,128]{3,2,1,0:T(8,128)}) custom-call(f32[3,16,32,128]{3,2,1,0:T(8,128)S(1)} %get-tuple-element.12.v_in, f32[6,16,32,128]{3,2,1,0:T(8,128)S(1)} %get-tuple-element.13.s_in, f32[6,16,32,128]{3,2,1,0:T(8,128)S(1)} %get-tuple-element.14.m_in, ...), custom_call_target="tpu_custom_call" | custom-call | tf_op jit(solution)/shard_map/pallas_call | solution.py:652
